TPU v7x, 32 devices: a whole 2x2x4 slice. The times are simulated.
32 devices in a mesh: grp: 2 (over y), row: 4 (over z), col: 4 (over x, core).
Axes of the slice: x: 2, y: 2, z: 4, core: 2. Of those that a mesh axis runs over, the one named last changes fastest.
Arguments:
- src_raw: bfloat16 [8, 2, 512, 1024], P(('grp', 'row'), None, 'col'), parts along dimension 0, may hold values from -36 to 36
- block_owner: int32 [4, 4], P('grp', 'col'), parts along dimension 0, may hold values from 0 to 3, as said below
- chan_order: int32 [4, 4, 128], P('grp', 'col'), parts along dimension 0, may hold values from 0 to 127, each once within a row
- rec_raw: bfloat16 [4, 16, 1024], P('grp', ('row', 'col')), parts along dimension 0, may hold values from -36 to 36
- fir_taps: bfloat16 [129], replicated, may hold values from -0.5 to 0.5
- stacks: float32 [1024, 1024], P(('grp', 'col'), 'row'), parts along dimension 0, may hold values from -6 to 6
Outputs:
- new_stacks: float32 [1024, 1024], P(('grp', 'col'), 'row'), parts along dimension 0
There are 2 independent parts, one for each index of `grp`. A program takes and returns all parts, laid end to end along the dimension named above; an argument that names none is the same for every part. Nothing has to cross between parts.
Inputs may be any that keep to these rules, and one draw needn't show every extreme that they name: block_owner[w, c] is the row index whose buffer holds column block c's traces in window w; 0 and 3 both occur in every draw.
All inputs are finite; a program needn't handle non-finite values.
Results may differ from a plain program's by a relative error of at most 0.0018.
Values may be sent and summed in bfloat16 or wider, within the bound.
No kernel may reach another device: no remote copies, remote signals or barrier semaphores. Data moves between devices by JAX's collectives and lax.ppermute only.
A program may use at most 64 MiB of HBM per device.

v0:
```python
import functools
import math

import jax
import jax.numpy as jnp
from jax import lax
from jax.experimental import pallas as pl
from jax.experimental.pallas import tpu as pltpu
from jax.sharding import PartitionSpec as P

LAGS = 64
LANES = 128
DIRECT_ROWS = 8
VMEM_GRANT = 16 * 2**20
VMEM = pl.BlockSpec(memory_space=pltpu.VMEM)
SMEM = pl.BlockSpec(memory_space=pltpu.SMEM)


def dot_nt(left, right):
    return lax.dot_general(left, right, (((1,), (1,)), ((), ())), preferred_element_type=jnp.float32)


def filter_rows(raw, band):
    blocks = raw.shape[1] // LANES
    halo = (band.shape[1] // LANES - 1) // 2
    out = []
    for block in range(blocks):
        low, high = max(block - halo, 0), min(block + halo + 1, blocks)
        first = low - (block - halo)
        taps = band[:, first * LANES : (first + high - low) * LANES]
        out.append(dot_nt(raw[:, low * LANES : high * LANES], taps))
    return jnp.concatenate(out[::-1], axis=1)


def source_kernel(owner_ref, order_ref, raw_ref, taps_ref, kept_ref, energy_ref, band_ref, row_ref):
    taps = taps_ref.shape[1]
    half = (taps - 1) // 2
    halo = pl.cdiv(half, LANES)
    row_ref[...] = jnp.zeros_like(row_ref)
    row_ref[:, 0:taps] = taps_ref[...].astype(jnp.float32)
    spread = jnp.broadcast_to(row_ref[...], (LANES, row_ref.shape[1]))
    band = pltpu.roll(spread, halo * LANES - half, 1, stride=1, stride_axis=0).astype(jnp.bfloat16)
    across = lax.broadcasted_iota(jnp.int32, (LANES, LANES), 0)
    down = lax.broadcasted_iota(jnp.int32, (LANES, LANES), 1)
    mirror = jnp.where(across + down == LANES - 1, 1.0, 0.0).astype(jnp.bfloat16)
    band = jnp.dot(mirror, band, preferred_element_type=jnp.float32).astype(jnp.bfloat16)
    band_ref[...] = band
    here = lax.axis_index("row")
    windows, count, _ = kept_ref.shape
    for window in range(windows):
        place = lax.broadcasted_iota(jnp.int32, (count, count), 0)
        order = jnp.where(owner_ref[window, 0] == here, order_ref[window], -1)
        chosen = jnp.where(place == order, 1.0, 0.0).T.astype(jnp.bfloat16)
        raw = jnp.dot(chosen, raw_ref[window], preferred_element_type=jnp.float32)
        kept = filter_rows(raw.astype(jnp.bfloat16), band).astype(jnp.bfloat16)
        kept_ref[window] = kept
        squares = jnp.square(kept.astype(jnp.float32))
        energy_ref[window] = jnp.sum(squares, axis=1, keepdims=True)


def prepare_sources(block_owner, chan_order, raw, fir_taps):
    windows, count, length = raw.shape
    taps = fir_taps.shape[0]
    width = LANES * (2 * pl.cdiv((taps - 1) // 2, LANES) + 1)
    return pl.pallas_call(
        source_kernel,
        out_shape=(
            jax.ShapeDtypeStruct((windows, count, length), jnp.bfloat16),
            jax.ShapeDtypeStruct((windows, count, 1), jnp.float32),
            jax.ShapeDtypeStruct((LANES, width), jnp.bfloat16),
        ),
        in_specs=[SMEM, VMEM, VMEM, VMEM],
        out_specs=(VMEM, VMEM, VMEM),
        scratch_shapes=[pltpu.VMEM((1, width), jnp.float32)],
        cost_estimate=pl.CostEstimate(
            flops=2 * windows * count * length * (count + width),
            bytes_accessed=4 * windows * count * length,
            transcendentals=0,
        ),
        compiler_params=pltpu.CompilerParams(vmem_limit_bytes=VMEM_GRANT),
        name="prepare_sources",
    )(block_owner, chan_order, raw, fir_taps.reshape(1, taps))


def pair_kernel(rec_ref, band_ref, kept_ref, energy_ref, out_ref, hankel_ref):
    receivers, windows, length = rec_ref.shape
    rows = receivers * windows
    raw = jnp.concatenate([rec_ref[q].astype(jnp.float32) for q in range(receivers)], axis=0)
    rec = filter_rows(raw.astype(jnp.bfloat16), band_ref[...])
    rec = rec.astype(jnp.bfloat16).astype(jnp.float32)
    rec_energy = jnp.sum(jnp.square(rec), axis=1, keepdims=True)
    padded = jnp.concatenate([rec, jnp.zeros((rows, LANES), jnp.float32)], axis=1)
    width = length + LANES
    for window in range(windows):
        for q in range(receivers):
            at = q * windows + window
            spread = jnp.broadcast_to(padded[at : at + 1], (LAGS, width))
            shifted = pltpu.roll(spread, width - LAGS // 2, 1, stride=1, stride_axis=0)
            hankel_ref[window, q * LAGS : (q + 1) * LAGS] = shifted[:, :length].astype(jnp.bfloat16)
    lane = lax.broadcasted_iota(jnp.int32, (rows, receivers * LAGS), 1) // LAGS
    row = lax.broadcasted_iota(jnp.int32, (rows, receivers * LAGS), 0)
    total = None
    for window in range(windows):
        own = jnp.where(row == lane * windows + window, rec_energy, 0.0)
        across = jnp.sum(own, axis=0, keepdims=True)
        lagged = dot_nt(kept_ref[window], hankel_ref[window])
        ratio = lagged * lax.rsqrt(energy_ref[window] * across + 1e-06)
        term = jnp.tanh(0.5 * math.sqrt(length) * ratio)
        total = term if total is None else total + term
    out_ref[...] = total.astype(out_ref.dtype)


def pair_terms(rec, band, kept, energy, dtype):
    receivers, windows, length = rec.shape
    count = kept.shape[1]
    return pl.pallas_call(
        pair_kernel,
        out_shape=jax.ShapeDtypeStruct((count, receivers * LAGS), dtype),
        in_specs=[VMEM] * 4,
        out_specs=VMEM,
        scratch_shapes=[pltpu.VMEM((windows, receivers * LAGS, length), jnp.bfloat16)],
        cost_estimate=pl.CostEstimate(
            flops=2 * windows * count * length * receivers * LAGS,
            bytes_accessed=4 * windows * count * length,
            transcendentals=windows * count * receivers * LAGS,
        ),
        compiler_params=pltpu.CompilerParams(vmem_limit_bytes=VMEM_GRANT),
        name="pair_terms",
    )(rec, band, kept, energy)


def gather_columns(piece, columns):
    here = lax.axis_index("col")
    if columns & (columns - 1):
        return lax.all_gather(piece, "col", axis=0, tiled=True)
    bit = 1
    while bit < columns:
        other = lax.ppermute(piece, "col", [(i, i ^ bit) for i in range(columns)])
        mine_first = (here & bit) == 0
        piece = jnp.concatenate(
            [jnp.where(mine_first, piece, other), jnp.where(mine_first, other, piece)], axis=0
        )
        bit *= 2
    return piece


def shards(mesh_shape, src_raw, block_owner, chan_order, rec_raw, fir_taps, stacks):
    rows, columns = mesh_shape["row"], mesh_shape["col"]
    kept, energy, band = prepare_sources(block_owner, chan_order, src_raw[0], fir_taps)
    receivers = gather_columns(jnp.swapaxes(rec_raw, 0, 1), columns)
    terms = functools.partial(pair_terms, band=band, kept=kept, energy=energy)
    if rows > DIRECT_ROWS:
        everyone = lax.all_gather(receivers, "row", axis=0)
        parts = lax.map(lambda rec: terms(rec, dtype=jnp.bfloat16), everyone)
        parts = lax.all_to_all(parts, "row", 0, 0, tiled=True)
        return stacks + jnp.sum(parts.astype(jnp.float32), axis=0)

    def partner(i, step):
        return i ^ step if rows & (rows - 1) == 0 else (i + step) % rows

    order = range(rows - 1, 0, -1)
    arrived = {}
    for step in order:
        pairs = [(partner(i, step), i) for i in range(rows)]
        arrived[step] = lax.ppermute(receivers, "row", pairs)
    parts = []
    for step in order:
        pairs = [(i, partner(i, step)) for i in range(rows)]
        parts.append(lax.ppermute(terms(arrived[step], dtype=jnp.bfloat16), "row", pairs))
    total = stacks + terms(receivers, dtype=jnp.float32)
    for part in parts:
        total = total + part.astype(jnp.float32)
    return total


def solution(mesh):
    in_specs = (
        P(("grp", "row"), None, "col", None),
        P("grp", "col"),
        P("grp", "col", None),
        P("grp", ("row", "col"), None),
        P(),
        P(("grp", "col"), "row"),
    )
    out_specs = P(("grp", "col"), "row")
    body = functools.partial(shards, dict(mesh.shape))
    return jax.shard_map(body, mesh=mesh, in_specs=in_specs, out_specs=out_specs, check_vma=False)
```

profile of v0, /device:TPU:0, one launch (start us, length us, event | category | flops | bytes accessed | tf_op | source)
XLA Modules:
  0.0 25.9 jit_solution(3529647601339358401)
XLA Ops:
  0.0 0.5 %collective-permute-start = (bf16[1,2,1024]{2,1,0:T(2,128)(2,1)}, bf16[1,2,1024]{2,1,0:T(2,128)(2,1)S(1)}, u32[]{:S(2)}, u32[]{:S(2)}) collective-permute-start(bf16[1,2,1024]{2,1,0:T(2,128)(2,1)} %bitcast.5), channel_id=1, source_target_pairs={{0,1},{1,0},{2,3},{3,2},{4,5},{5,4},{6,7},{7,6},{8,9},{9,8},{10,11... | collective-permute-start | bytes 12296 | tf_op jit(solution)/shard_map/ppermute | solution.py:138
  0.5 0.0 copy-start.3
  0.5 1.0 %collective-permute-done = bf16[1,2,1024]{2,1,0:T(2,128)(2,1)S(1)} collective-permute-done((bf16[1,2,1024]{2,1,0:T(2,128)(2,1)}, bf16[1,2,1024]{2,1,0:T(2,128)(2,1)S(1)}, u32[]{:S(2)}, u32[]{:S(2)}) %collective-permute-start) | collective-permute-done | bytes 4128 | tf_op jit(solution)/shard_map/ppermute | solution.py:138
  1.5 0.0 copy-done.3
  1.6 2.9 %collective-permute-start.1 = (bf16[2,2,1024]{2,1,0:T(2,128)(2,1)S(1)}, bf16[2,2,1024]{2,1,0:T(2,128)(2,1)S(1)}, u32[]{:S(2)}, u32[]{:S(2)}) collective-permute-start(bf16[2,2,1024]{2,1,0:T(2,128)(2,1)S(1)} %pad_maximum_fusion.1), channel_id=1, source_target_pairs={{0,2},{1,3},{2,0},{3,1},{4,6},{5,7},{6,4},{7,5},{8,10},{9,11},{10,... | collective-permute-start | bytes 24584 | tf_op jit(solution)/shard_map/ppermute | solution.py:138
  4.5 0.7 %copy-done.4 = s32[2,1]{0,1:T(1,128)S(1)} copy-done((s32[2,1]{0,1:T(1,128)S(1)}, s32[2,1]{0,1:T(1,128)}, u32[]{:S(2)}) %copy-start.4) | copy-done | bytes 32
  5.1 0.1 copy.7.owner_ref
  5.2 0.6 %copy-done.5 = bf16[129]{0:T(256)(128)(2,1)S(1)} copy-done((bf16[129]{0:T(256)(128)(2,1)S(1)}, bf16[129]{0:T(256)(128)(2,1)}, u32[]{:S(2)}) %copy-start.5) | copy-done | bytes 282
  5.8 0.3 %collective-permute-done.1 = bf16[2,2,1024]{2,1,0:T(2,128)(2,1)S(1)} collective-permute-done((bf16[2,2,1024]{2,1,0:T(2,128)(2,1)S(1)}, bf16[2,2,1024]{2,1,0:T(2,128)(2,1)S(1)}, u32[]{:S(2)}, u32[]{:S(2)}) %collective-permute-start.1) | collective-permute-done | bytes 8224 | tf_op jit(solution)/shard_map/ppermute | solution.py:138
  6.1 0.0 copy-start.1
  6.2 3.2 %collective-permute-start.4 = (bf16[4,2,1024]{2,1,0:T(2,128)(2,1)S(1)}, bf16[4,2,1024]{2,1,0:T(2,128)(2,1)S(1)}, u32[]{:S(2)}, u32[]{:S(2)}) collective-permute-start(bf16[4,2,1024]{2,1,0:T(2,128)(2,1)S(1)} %pad_maximum_fusion.rec_ref), channel_id=1, source_target_pairs={{8,0},{12,4},{0,8},{4,12},{9,1},{13,5},{1,9},{5,13},{10,2},{14,6},... | collective-permute-start | bytes 49160 | tf_op jit(solution)/shard_map/ppermute | solution.py:165
  9.3 1.3 %collective-permute-start.2 = (bf16[4,2,1024]{2,1,0:T(2,128)(2,1)S(1)}, bf16[4,2,1024]{2,1,0:T(2,128)(2,1)S(1)}, u32[]{:S(2)}, u32[]{:S(2)}) collective-permute-start(bf16[4,2,1024]{2,1,0:T(2,128)(2,1)S(1)} %pad_maximum_fusion.rec_ref), channel_id=1, source_target_pairs={{12,0},{8,4},{4,8},{0,12},{13,1},{9,5},{5,9},{1,13},{14,2},{10,6},... | collective-permute-start | bytes 49160 | tf_op jit(solution)/shard_map/ppermute | solution.py:165
  10.7 0.0 copy-done.1
  10.7 1.0 %copy-done = bf16[1,2,128,1024]{3,2,1,0:T(8,128)(2,1)S(1)} copy-done((bf16[1,2,128,1024]{3,2,1,0:T(8,128)(2,1)S(1)}, bf16[1,2,128,1024]{3,2,1,0:T(8,128)(2,1)}, u32[]{:S(2)}) %copy-start) | copy-done | bytes 524312
  11.7 1.7 %prepare_sources.1 = (bf16[2,128,1024]{2,1,0:T(8,128)(2,1)S(1)}, f32[2,128,1]{2,1,0:T(8,128)S(1)}, bf16[128,384]{1,0:T(8,128)(2,1)S(1)}) custom-call(s32[2,1]{1,0:T(2,128)S(1)} %copy.7.owner_ref, s32[2,1,128]{2,1,0:T(1,128)S(1)} %copy-done.1, bf16[2,128,1024]{2,1,0:T(8,128)(2,1)S(1)} %bitcast.4, bf16[1,129]{1,0:T(2,128)(2,1)S(1)} %reshape.3.taps_ref), custom_call_target="tpu_custom_call" | custom-call | flops 268435456 | bytes 1048576 | tf_op jit(solution)/shard_map/prepare_sources/pallas_call | solution.py:65
  13.5 0.3 %collective-permute-start.6 = (bf16[4,2,1024]{2,1,0:T(2,128)(2,1)S(1)}, bf16[4,2,1024]{2,1,0:T(2,128)(2,1)S(1)}, u32[]{:S(2)}, u32[]{:S(2)}) collective-permute-start(bf16[4,2,1024]{2,1,0:T(2,128)(2,1)S(1)} %pad_maximum_fusion.rec_ref), channel_id=1, source_target_pairs={{4,0},{0,4},{12,8},{8,12},{5,1},{1,5},{13,9},{9,13},{6,2},{2,6},{1... | collective-permute-start | bytes 49160 | tf_op jit(solution)/shard_map/ppermute | solution.py:165
  13.8 1.2 %collective-permute-done.2.rec_ref = bf16[4,2,1024]{2,1,0:T(2,128)(2,1)S(1)} collective-permute-done((bf16[4,2,1024]{2,1,0:T(2,128)(2,1)S(1)}, bf16[4,2,1024]{2,1,0:T(2,128)(2,1)S(1)}, u32[]{:S(2)}, u32[]{:S(2)}) %collective-permute-start.2) | collective-permute-done | bytes 16416 | tf_op jit(solution)/shard_map/ppermute | solution.py:165
  15.0 1.0 %pair_terms.5 = bf16[128,256]{1,0:T(8,128)(2,1)S(1)} custom-call(bf16[4,2,1024]{2,1,0:T(2,128)(2,1)S(1)} %collective-permute-done.2.rec_ref, bf16[128,384]{1,0:T(8,128)(2,1)S(1)} %get-tuple-element.8.band_ref, bf16[2,128,1024]{2,1,0:T(8,128)(2,1)S(1)} %get-tuple-element.9.kept_ref, f32[2,128,1]{2,1,0:T(8,128)S(1)} %get-tuple-element.10.energy_ref), custom_call_target="tpu_custom_call" | custom-call | flops 134217728 | bytes 1048576 | tf_op jit(solution)/shard_map/pair_terms/pallas_call | solution.py:116
  16.0 1.8 %collective-permute-start.3 = (bf16[128,256]{1,0:T(8,128)(2,1)S(1)}, bf16[128,256]{1,0:T(8,128)(2,1)S(1)}, u32[]{:S(2)}, u32[]{:S(2)}) collective-permute-start(bf16[128,256]{1,0:T(8,128)(2,1)S(1)} %pair_terms.5), channel_id=1, source_target_pairs={{0,12},{4,8},{8,4},{12,0},{1,13},{5,9},{9,5},{13,1},{2,14},{6,10},... | collective-permute-start | bytes 196616 | tf_op jit(solution)/shard_map/ppermute | solution.py:169
  17.7 0.0 collective-permute-done.4.rec_ref
  17.7 1.0 %pair_terms.6 = bf16[128,256]{1,0:T(8,128)(2,1)S(1)} custom-call(bf16[4,2,1024]{2,1,0:T(2,128)(2,1)S(1)} %collective-permute-done.4.rec_ref, bf16[128,384]{1,0:T(8,128)(2,1)S(1)} %get-tuple-element.8.band_ref, bf16[2,128,1024]{2,1,0:T(8,128)(2,1)S(1)} %get-tuple-element.9.kept_ref, f32[2,128,1]{2,1,0:T(8,128)S(1)} %get-tuple-element.10.energy_ref), custom_call_target="tpu_custom_call" | custom-call | flops 134217728 | bytes 1048576 | tf_op jit(solution)/shard_map/pair_terms/pallas_call | solution.py:116
  18.7 0.4 %collective-permute-start.5 = (bf16[128,256]{1,0:T(8,128)(2,1)S(1)}, bf16[128,256]{1,0:T(8,128)(2,1)S(1)}, u32[]{:S(2)}, u32[]{:S(2)}) collective-permute-start(bf16[128,256]{1,0:T(8,128)(2,1)S(1)} %pair_terms.6), channel_id=1, source_target_pairs={{0,8},{4,12},{8,0},{12,4},{1,9},{5,13},{9,1},{13,5},{2,10},{6,14},... | collective-permute-start | bytes 196616 | tf_op jit(solution)/shard_map/ppermute | solution.py:169
  19.1 0.0 collective-permute-done.6.rec_ref
  19.1 1.0 %pair_terms.7 = bf16[128,256]{1,0:T(8,128)(2,1)S(1)} custom-call(bf16[4,2,1024]{2,1,0:T(2,128)(2,1)S(1)} %collective-permute-done.6.rec_ref, bf16[128,384]{1,0:T(8,128)(2,1)S(1)} %get-tuple-element.8.band_ref, bf16[2,128,1024]{2,1,0:T(8,128)(2,1)S(1)} %get-tuple-element.9.kept_ref, f32[2,128,1]{2,1,0:T(8,128)S(1)} %get-tuple-element.10.energy_ref), custom_call_target="tpu_custom_call" | custom-call | flops 134217728 | bytes 1048576 | tf_op jit(solution)/shard_map/pair_terms/pallas_call | solution.py:116
  20.1 0.0 copy-start.2
  20.1 2.4 %collective-permute-start.7 = (bf16[128,256]{1,0:T(8,128)(2,1)S(1)}, bf16[128,256]{1,0:T(8,128)(2,1)S(1)}, u32[]{:S(2)}, u32[]{:S(2)}) collective-permute-start(bf16[128,256]{1,0:T(8,128)(2,1)S(1)} %pair_terms.7), channel_id=1, source_target_pairs={{0,4},{4,0},{8,12},{12,8},{1,5},{5,1},{9,13},{13,9},{2,6},{6,2},{1... | collective-permute-start | bytes 196616 | tf_op jit(solution)/shard_map/ppermute | solution.py:169
  22.5 1.0 %pair_terms.4 = f32[128,256]{1,0:T(8,128)S(1)} custom-call(bf16[4,2,1024]{2,1,0:T(2,128)(2,1)S(1)} %pad_maximum_fusion.rec_ref, bf16[128,384]{1,0:T(8,128)(2,1)S(1)} %get-tuple-element.8.band_ref, bf16[2,128,1024]{2,1,0:T(8,128)(2,1)S(1)} %get-tuple-element.9.kept_ref, f32[2,128,1]{2,1,0:T(8,128)S(1)} %get-tuple-element.10.energy_ref), custom_call_target="tpu_custom_call" | custom-call | flops 134217728 | bytes 1048576 | tf_op jit(solution)/shard_map/pair_terms/pallas_call | solution.py:116
  23.5 0.0 collective-permute-done.3
  23.5 1.1 %collective-permute-done.5 = bf16[128,256]{1,0:T(8,128)(2,1)S(1)} collective-permute-done((bf16[128,256]{1,0:T(8,128)(2,1)S(1)}, bf16[128,256]{1,0:T(8,128)(2,1)S(1)}, u32[]{:S(2)}, u32[]{:S(2)}) %collective-permute-start.5) | collective-permute-done | bytes 65568 | tf_op jit(solution)/shard_map/ppermute | solution.py:169
  24.6 0.7 %collective-permute-done.7 = bf16[128,256]{1,0:T(8,128)(2,1)S(1)} collective-permute-done((bf16[128,256]{1,0:T(8,128)(2,1)S(1)}, bf16[128,256]{1,0:T(8,128)(2,1)S(1)}, u32[]{:S(2)}, u32[]{:S(2)}) %collective-permute-start.7) | collective-permute-done | bytes 65568 | tf_op jit(solution)/shard_map/ppermute | solution.py:169
  25.3 0.0 copy-done.2
  25.3 0.7 %convert_add_fusion = f32[128,256]{1,0:T(8,128)} fusion(bf16[128,256]{1,0:T(8,128)(2,1)S(1)} %collective-permute-done.7, bf16[128,256]{1,0:T(8,128)(2,1)S(1)} %collective-permute-done.5, bf16[128,256]{1,0:T(8,128)(2,1)S(1)} %collective-permute-done.3, f32[128,256]{1,0:T(8,128)S(1)} %copy-done.2, f32[128,256]{1,0:T(8,128)S(1)} %pair_terms.4), kind=kLoop, calls=%fused_computation | loop fusion | flops 229376 | bytes 589824 | tf_op jit(solution)/shard_map/add | solution.py:172
  (8 shorter events, 0.1 us)
Async XLA Ops:
  0.0 1.5 %collective-permute-start = (bf16[1,2,1024]{2,1,0:T(2,128)(2,1)}, bf16[1,2,1024]{2,1,0:T(2,128)(2,1)S(1)}, u32[]{:S(2)}, u32[]{:S(2)}) collective-permute-start(bf16[1,2,1024]{2,1,0:T(2,128)(2,1)} %bitcast.5), channel_id=1, source_target_pairs={{0,1},{1,0},{2,3},{3,2},{4,5},{5,4},{6,7},{7,6},{8,9},{9,8},{10,11... | collective-permute-start | bytes 12296 | tf_op jit(solution)/shard_map/ppermute | solution.py:138
  0.5 1.0 %copy-start.3 = (bf16[2,1,1024]{2,0,1:T(2,128)(2,1)S(1)}, bf16[2,1,1024]{2,0,1:T(2,128)(2,1)}, u32[]{:S(2)}) copy-start(bf16[2,1,1024]{2,0,1:T(2,128)(2,1)} %param.9) | copy-start | bytes 12292
  1.6 4.5 %collective-permute-start.1 = (bf16[2,2,1024]{2,1,0:T(2,128)(2,1)S(1)}, bf16[2,2,1024]{2,1,0:T(2,128)(2,1)S(1)}, u32[]{:S(2)}, u32[]{:S(2)}) collective-permute-start(bf16[2,2,1024]{2,1,0:T(2,128)(2,1)S(1)} %pad_maximum_fusion.1), channel_id=1, source_target_pairs={{0,2},{1,3},{2,0},{3,1},{4,6},{5,7},{6,4},{7,5},{8,10},{9,11},{10,... | collective-permute-start | bytes 24584 | tf_op jit(solution)/shard_map/ppermute | solution.py:138
  4.5 0.7 %copy-start.4 = (s32[2,1]{0,1:T(1,128)S(1)}, s32[2,1]{0,1:T(1,128)}, u32[]{:S(2)}) copy-start(s32[2,1]{0,1:T(1,128)} %param.7) | copy-start | bytes 28
  5.1 0.7 %copy-start.5 = (bf16[129]{0:T(256)(128)(2,1)S(1)}, bf16[129]{0:T(256)(128)(2,1)}, u32[]{:S(2)}) copy-start(bf16[129]{0:T(256)(128)(2,1)} %param.10) | copy-start | bytes 778
  6.1 4.5 %copy-start.1 = (s32[2,1,128]{2,1,0:T(1,128)S(1)}, s32[2,1,128]{2,1,0:T(1,128)}, u32[]{:S(2)}) copy-start(s32[2,1,128]{2,1,0:T(1,128)} %order_ref.1) | copy-start | bytes 3076
  6.2 11.6 %collective-permute-start.4 = (bf16[4,2,1024]{2,1,0:T(2,128)(2,1)S(1)}, bf16[4,2,1024]{2,1,0:T(2,128)(2,1)S(1)}, u32[]{:S(2)}, u32[]{:S(2)}) collective-permute-start(bf16[4,2,1024]{2,1,0:T(2,128)(2,1)S(1)} %pad_maximum_fusion.rec_ref), channel_id=1, source_target_pairs={{8,0},{12,4},{0,8},{4,12},{9,1},{13,5},{1,9},{5,13},{10,2},{14,6},... | collective-permute-start | bytes 49160 | tf_op jit(solution)/shard_map/ppermute | solution.py:165
  9.3 5.6 %collective-permute-start.2 = (bf16[4,2,1024]{2,1,0:T(2,128)(2,1)S(1)}, bf16[4,2,1024]{2,1,0:T(2,128)(2,1)S(1)}, u32[]{:S(2)}, u32[]{:S(2)}) collective-permute-start(bf16[4,2,1024]{2,1,0:T(2,128)(2,1)S(1)} %pad_maximum_fusion.rec_ref), channel_id=1, source_target_pairs={{12,0},{8,4},{4,8},{0,12},{13,1},{9,5},{5,9},{1,13},{14,2},{10,6},... | collective-permute-start | bytes 49160 | tf_op jit(solution)/shard_map/ppermute | solution.py:165
  10.7 1.0 %copy-start = (bf16[1,2,128,1024]{3,2,1,0:T(8,128)(2,1)S(1)}, bf16[1,2,128,1024]{3,2,1,0:T(8,128)(2,1)}, u32[]{:S(2)}) copy-start(bf16[1,2,128,1024]{3,2,1,0:T(8,128)(2,1)} %param.6) | copy-start | bytes 1572868
  13.5 5.7 %collective-permute-start.6 = (bf16[4,2,1024]{2,1,0:T(2,128)(2,1)S(1)}, bf16[4,2,1024]{2,1,0:T(2,128)(2,1)S(1)}, u32[]{:S(2)}, u32[]{:S(2)}) collective-permute-start(bf16[4,2,1024]{2,1,0:T(2,128)(2,1)S(1)} %pad_maximum_fusion.rec_ref), channel_id=1, source_target_pairs={{4,0},{0,4},{12,8},{8,12},{5,1},{1,5},{13,9},{9,13},{6,2},{2,6},{1... | collective-permute-start | bytes 49160 | tf_op jit(solution)/shard_map/ppermute | solution.py:165
  16.0 7.5 %collective-permute-start.3 = (bf16[128,256]{1,0:T(8,128)(2,1)S(1)}, bf16[128,256]{1,0:T(8,128)(2,1)S(1)}, u32[]{:S(2)}, u32[]{:S(2)}) collective-permute-start(bf16[128,256]{1,0:T(8,128)(2,1)S(1)} %pair_terms.5), channel_id=1, source_target_pairs={{0,12},{4,8},{8,4},{12,0},{1,13},{5,9},{9,5},{13,1},{2,14},{6,10},... | collective-permute-start | bytes 196616 | tf_op jit(solution)/shard_map/ppermute | solution.py:169
  18.7 5.9 %collective-permute-start.5 = (bf16[128,256]{1,0:T(8,128)(2,1)S(1)}, bf16[128,256]{1,0:T(8,128)(2,1)S(1)}, u32[]{:S(2)}, u32[]{:S(2)}) collective-permute-start(bf16[128,256]{1,0:T(8,128)(2,1)S(1)} %pair_terms.6), channel_id=1, source_target_pairs={{0,8},{4,12},{8,0},{12,4},{1,9},{5,13},{9,1},{13,5},{2,10},{6,14},... | collective-permute-start | bytes 196616 | tf_op jit(solution)/shard_map/ppermute | solution.py:169
  20.1 5.1 %copy-start.2 = (f32[128,256]{1,0:T(8,128)S(1)}, f32[128,256]{1,0:T(8,128)}, u32[]{:S(2)}) copy-start(f32[128,256]{1,0:T(8,128)} %param.11) | copy-start | bytes 393220
  20.1 5.1 %collective-permute-start.7 = (bf16[128,256]{1,0:T(8,128)(2,1)S(1)}, bf16[128,256]{1,0:T(8,128)(2,1)S(1)}, u32[]{:S(2)}, u32[]{:S(2)}) collective-permute-start(bf16[128,256]{1,0:T(8,128)(2,1)S(1)} %pair_terms.7), channel_id=1, source_target_pairs={{0,4},{4,0},{8,12},{12,8},{1,5},{5,1},{9,13},{13,9},{2,6},{6,2},{1... | collective-permute-start | bytes 196616 | tf_op jit(solution)/shard_map/ppermute | solution.py:169
where the time goes:
time: 26.1 us; the launch traced here: 25.9 us
  starting transfers between devices  12.8 us (49%)
  Pallas kernels  5.63 us (22%)
  waiting for transfers between devices  4.31 us (17%)
  local copies, waits for them, and re-layouts  2.37 us (9%)
  other arithmetic  0.77 us (3%)
    ppermute x3, starting transfers between devices, shards(): arrived[step] = lax.ppermute(receivers, 'row', pairs)  4.82 us
    ppermute x3, starting transfers between devices, shards(): lax.ppermute(terms(arrived[step], dtype=jnp.bfloat16), 'row', pairs)  4.58 us
    pallas_call x4, Pallas kernels, pair_terms(): pl.pallas_call(pair_kernel, out_shape=jax.ShapeDtypeStruct((count, receiv...  3.9 us
    ppermute x2, starting transfers between devices, gather_columns(): other = lax.ppermute(piece, 'col', [(i, i ^ bit) for i in range(columns)])  3.38 us
    unnamed x13, local copies, waits for them, and re-layouts  2.37 us
    ppermute x3, waiting for transfers between devices, shards(): lax.ppermute(terms(arrived[step], dtype=jnp.bfloat16), 'row', pairs)  1.74 us
    pallas_call x1, Pallas kernels, prepare_sources(): pl.pallas_call(source_kernel, out_shape=(jax.ShapeDtypeStruct((windows, c...  1.74 us
    ppermute x2, waiting for transfers between devices, gather_columns(): other = lax.ppermute(piece, 'col', [(i, i ^ bit) for i in range(columns)])  1.35 us
  transfers between devices with their start and end apart: 8, of which 5 were waited for; matrix products, arithmetic and copies ran while one was open for 0% of the time, Pallas kernels for 22%

commit v1 on v0

--- a/solution.py
+++ b/solution.py
@@ -13,7 +13,11 @@
 DIRECT_ROWS = 8
 VMEM_GRANT = 16 * 2**20
 VMEM = pl.BlockSpec(memory_space=pltpu.VMEM)
-SMEM = pl.BlockSpec(memory_space=pltpu.SMEM)
+HBM = pl.BlockSpec(memory_space=pltpu.HBM)
+
+
+def in_hbm(value):
+    return pltpu.with_memory_space_constraint(value, pltpu.HBM)
 
 
 def dot_nt(left, right):
@@ -21,36 +25,65 @@
 
 
 def filter_rows(raw, band):
-    blocks = raw.shape[1] // LANES
-    halo = (band.shape[1] // LANES - 1) // 2
-    out = []
-    for block in range(blocks):
-        low, high = max(block - halo, 0), min(block + halo + 1, blocks)
-        first = low - (block - halo)
-        taps = band[:, first * LANES : (first + high - low) * LANES]
-        out.append(dot_nt(raw[:, low * LANES : high * LANES], taps))
-    return jnp.concatenate(out[::-1], axis=1)
-
-
-def source_kernel(owner_ref, order_ref, raw_ref, taps_ref, kept_ref, energy_ref, band_ref, row_ref):
+    rows, length = raw.shape
+    block, width = band.shape
+    halo = (width - block) // 2
+    edge = jnp.zeros((rows, halo), raw.dtype)
+    padded = jnp.concatenate([edge, raw, edge], axis=1)
+    starts = range(0, length, block)
+    stacked = jnp.concatenate([padded[:, start : start + width] for start in starts], axis=0)
+    out = dot_nt(stacked.astype(jnp.bfloat16), band)
+    pieces = [out[i * rows : (i + 1) * rows] for i in range(len(starts))]
+    return jnp.concatenate(pieces[::-1], axis=1)
+
+
+def source_kernel(
+    owner_hbm,
+    order_hbm,
+    raw_hbm,
+    taps_ref,
+    kept_ref,
+    energy_ref,
+    band_ref,
+    owner_ref,
+    order_ref,
+    raw_ref,
+    row_ref,
+    arrived,
+):
+    windows, count, _ = kept_ref.shape
+    owner_copy = pltpu.make_async_copy(owner_hbm, owner_ref, arrived.at[windows])
+    order_copy = pltpu.make_async_copy(order_hbm, order_ref, arrived.at[windows + 1])
+    copies = [
+        pltpu.make_async_copy(raw_hbm.at[window], raw_ref.at[window], arrived.at[window])
+        for window in range(windows)
+    ]
+    for copy in (owner_copy, order_copy, *copies):
+        copy.start()
     taps = taps_ref.shape[1]
     half = (taps - 1) // 2
-    halo = pl.cdiv(half, LANES)
+    block, width = band_ref.shape
     row_ref[...] = jnp.zeros_like(row_ref)
     row_ref[:, 0:taps] = taps_ref[...].astype(jnp.float32)
-    spread = jnp.broadcast_to(row_ref[...], (LANES, row_ref.shape[1]))
-    band = pltpu.roll(spread, halo * LANES - half, 1, stride=1, stride_axis=0).astype(jnp.bfloat16)
+    spread = jnp.broadcast_to(row_ref[...], (LANES, width - LANES))
+    part = pltpu.roll(spread, (width - block) // 2 - half, 1, stride=1, stride_axis=0)
     across = lax.broadcasted_iota(jnp.int32, (LANES, LANES), 0)
     down = lax.broadcasted_iota(jnp.int32, (LANES, LANES), 1)
     mirror = jnp.where(across + down == LANES - 1, 1.0, 0.0).astype(jnp.bfloat16)
-    band = jnp.dot(mirror, band, preferred_element_type=jnp.float32).astype(jnp.bfloat16)
+    part = jnp.dot(mirror, part.astype(jnp.bfloat16), preferred_element_type=jnp.float32)
+    empty = jnp.zeros((LANES, LANES), jnp.float32)
+    upper = jnp.concatenate([empty, part], axis=1)
+    lower = jnp.concatenate([part, empty], axis=1)
+    band = jnp.concatenate([upper, lower], axis=0).astype(jnp.bfloat16)
     band_ref[...] = band
     here = lax.axis_index("row")
-    windows, count, _ = kept_ref.shape
+    owner_copy.wait()
+    order_copy.wait()
     for window in range(windows):
         place = lax.broadcasted_iota(jnp.int32, (count, count), 0)
-        order = jnp.where(owner_ref[window, 0] == here, order_ref[window], -1)
+        order = jnp.where(owner_ref[0, window] == here, order_ref[window], -1)
         chosen = jnp.where(place == order, 1.0, 0.0).T.astype(jnp.bfloat16)
+        copies[window].wait()
         raw = jnp.dot(chosen, raw_ref[window], preferred_element_type=jnp.float32)
         kept = filter_rows(raw.astype(jnp.bfloat16), band).astype(jnp.bfloat16)
         kept_ref[window] = kept
@@ -61,17 +94,24 @@
 def prepare_sources(block_owner, chan_order, raw, fir_taps):
     windows, count, length = raw.shape
     taps = fir_taps.shape[0]
-    width = LANES * (2 * pl.cdiv((taps - 1) // 2, LANES) + 1)
+    block = 2 * LANES
+    width = block + 2 * LANES * pl.cdiv((taps - 1) // 2, LANES)
     return pl.pallas_call(
         source_kernel,
         out_shape=(
             jax.ShapeDtypeStruct((windows, count, length), jnp.bfloat16),
             jax.ShapeDtypeStruct((windows, count, 1), jnp.float32),
-            jax.ShapeDtypeStruct((LANES, width), jnp.bfloat16),
+            jax.ShapeDtypeStruct((block, width), jnp.bfloat16),
         ),
-        in_specs=[SMEM, VMEM, VMEM, VMEM],
+        in_specs=[HBM, HBM, HBM, VMEM],
         out_specs=(VMEM, VMEM, VMEM),
-        scratch_shapes=[pltpu.VMEM((1, width), jnp.float32)],
+        scratch_shapes=[
+            pltpu.SMEM((1, windows), jnp.int32),
+            pltpu.VMEM((windows, 1, count), jnp.int32),
+            pltpu.VMEM((windows, count, length), jnp.bfloat16),
+            pltpu.VMEM((1, width - LANES), jnp.float32),
+            pltpu.SemaphoreType.DMA((windows + 2,)),
+        ],
         cost_estimate=pl.CostEstimate(
             flops=2 * windows * count * length * (count + width),
             bytes_accessed=4 * windows * count * length,
@@ -79,14 +119,14 @@
         ),
         compiler_params=pltpu.CompilerParams(vmem_limit_bytes=VMEM_GRANT),
         name="prepare_sources",
-    )(block_owner, chan_order, raw, fir_taps.reshape(1, taps))
+    )(in_hbm(block_owner.T), in_hbm(chan_order), in_hbm(raw), fir_taps.reshape(1, taps))
 
 
 def pair_kernel(rec_ref, band_ref, kept_ref, energy_ref, out_ref, hankel_ref):
     receivers, windows, length = rec_ref.shape
     rows = receivers * windows
     raw = jnp.concatenate([rec_ref[q].astype(jnp.float32) for q in range(receivers)], axis=0)
-    rec = filter_rows(raw.astype(jnp.bfloat16), band_ref[...])
+    rec = filter_rows(raw, band_ref[...])
     rec = rec.astype(jnp.bfloat16).astype(jnp.float32)
     rec_energy = jnp.sum(jnp.square(rec), axis=1, keepdims=True)
     padded = jnp.concatenate([rec, jnp.zeros((rows, LANES), jnp.float32)], axis=1)
@@ -148,6 +188,7 @@
     rows, columns = mesh_shape["row"], mesh_shape["col"]
     kept, energy, band = prepare_sources(block_owner, chan_order, src_raw[0], fir_taps)
     receivers = gather_columns(jnp.swapaxes(rec_raw, 0, 1), columns)
+    receivers, kept, energy, band = lax.optimization_barrier((receivers, kept, energy, band))
     terms = functools.partial(pair_terms, band=band, kept=kept, energy=energy)
     if rows > DIRECT_ROWS:
         everyone = lax.all_gather(receivers, "row", axis=0)
@@ -158,7 +199,7 @@
     def partner(i, step):
         return i ^ step if rows & (rows - 1) == 0 else (i + step) % rows
 
-    order = range(rows - 1, 0, -1)
+    order = [1, *range(rows - 1, 1, -1)]
     arrived = {}
     for step in order:
         pairs = [(partner(i, step), i) for i in range(rows)]

time: 26.1 us -> 23.8 us (0.912)
  local copies, waits for them, and re-layouts: 2.37 us -> 0.67 us
  starting transfers between devices: 12.8 us -> 12.1 us
    unnamed x13 -> x6, local copies, waits for them, and re-layouts: 2.37 us -> 0.66 us
    ppermute x3, waiting for transfers between devices: 1.74 us -> 3.26 us  [shards(): lax.ppermute(terms(arrived[step], dtype=jnp.bfloat16), 'row', pairs)]
    ppermute x2, waiting for transfers between devices: 1.35 us -> 0.38 us  [gather_columns(): other = lax.ppermute(piece, 'col', [(i, i ^ bit) for i in range(columns)])]
    ppermute x3, waiting for transfers between devices: 1.23 us -> 0.58 us  [shards(): arrived[step] = lax.ppermute(receivers, 'row', pairs)]
    ppermute x3, starting transfers between devices: 4.82 us -> 4.24 us  [shards(): arrived[step] = lax.ppermute(receivers, 'row', pairs)]
    pallas_call x1, Pallas kernels: 1.74 us -> 2.29 us  [prepare_sources(): pl.pallas_call(source_kernel, out_shape=(jax.ShapeDtypeStruct((windows, c...]
    pallas_call x4, Pallas kernels: 3.9 us -> 3.49 us  [pair_terms(): pl.pallas_call(pair_kernel, out_shape=jax.ShapeDtypeStruct((count, receiv...]
  transfers between devices with their start and end apart: 8 -> 8, of which waited for: 5 -> 4; matrix products, arithmetic and copies ran while one was open for 0% -> 0% of each run, Pallas kernels for 22% -> 24%
where the time goes in v1:
time: 23.8 us; the launch traced here: 23.7 us
  starting transfers between devices  12.1 us (51%)
  Pallas kernels  5.78 us (24%)
  waiting for transfers between devices  4.21 us (18%)
  other arithmetic  0.77 us (3%)
  local copies, waits for them, and re-layouts  0.67 us (3%)
    ppermute x3, starting transfers between devices, shards(): lax.ppermute(terms(arrived[step], dtype=jnp.bfloat16), 'row', pairs)  4.52 us
    ppermute x3, starting transfers between devices, shards(): arrived[step] = lax.ppermute(receivers, 'row', pairs)  4.24 us
    pallas_call x4, Pallas kernels, pair_terms(): pl.pallas_call(pair_kernel, out_shape=jax.ShapeDtypeStruct((count, receiv...  3.49 us
    ppermute x2, starting transfers between devices, gather_columns(): other = lax.ppermute(piece, 'col', [(i, i ^ bit) for i in range(columns)])  3.38 us
    ppermute x3, waiting for transfers between devices, shards(): lax.ppermute(terms(arrived[step], dtype=jnp.bfloat16), 'row', pairs)  3.26 us
    pallas_call x1, Pallas kernels, prepare_sources(): pl.pallas_call(source_kernel, out_shape=(jax.ShapeDtypeStruct((windows, c...  2.29 us
    add x1, other arithmetic, shards(): total = total + part.astype(jnp.float32)  0.69 us
    unnamed x6, local copies, waits for them, and re-layouts  0.66 us
  transfers between devices with their start and end apart: 8, of which 4 were waited for; matrix products, arithmetic and copies ran while one was open for 0% of the time, Pallas kernels for 24%

profile of v1, /device:TPU:0, one launch (start us, length us, event | category | flops | bytes accessed | tf_op | source)
XLA Modules:
  0.0 23.7 jit_solution(2900561920183871862)
XLA Ops:
  0.0 0.5 %collective-permute-start = (bf16[1,2,1024]{2,1,0:T(2,128)(2,1)}, bf16[1,2,1024]{2,1,0:T(2,128)(2,1)S(1)}, u32[]{:S(2)}, u32[]{:S(2)}) collective-permute-start(bf16[1,2,1024]{2,1,0:T(2,128)(2,1)} %bitcast.5), channel_id=1, source_target_pairs={{0,1},{1,0},{2,3},{3,2},{4,5},{5,4},{6,7},{7,6},{8,9},{9,8},{10,11... | collective-permute-start | bytes 12296 | tf_op jit(solution)/shard_map/ppermute | solution.py:178
  0.5 0.0 copy-start.2
  0.5 0.0 copy-start.1
  0.5 0.7 %copy-done.2 = bf16[129]{0:T(256)(128)(2,1)S(1)} copy-done((bf16[129]{0:T(256)(128)(2,1)S(1)}, bf16[129]{0:T(256)(128)(2,1)}, u32[]{:S(2)}) %copy-start.2) | copy-done | bytes 282
  1.2 0.4 %collective-permute-done = bf16[1,2,1024]{2,1,0:T(2,128)(2,1)S(1)} collective-permute-done((bf16[1,2,1024]{2,1,0:T(2,128)(2,1)}, bf16[1,2,1024]{2,1,0:T(2,128)(2,1)S(1)}, u32[]{:S(2)}, u32[]{:S(2)}) %collective-permute-start) | collective-permute-done | bytes 4128 | tf_op jit(solution)/shard_map/ppermute | solution.py:178
  1.5 0.0 copy-done.1
  1.6 2.9 %collective-permute-start.1 = (bf16[2,2,1024]{2,1,0:T(2,128)(2,1)S(1)}, bf16[2,2,1024]{2,1,0:T(2,128)(2,1)S(1)}, u32[]{:S(2)}, u32[]{:S(2)}) collective-permute-start(bf16[2,2,1024]{2,1,0:T(2,128)(2,1)S(1)} %pad_maximum_fusion.1), channel_id=1, source_target_pairs={{0,2},{1,3},{2,0},{3,1},{4,6},{5,7},{6,4},{7,5},{8,10},{9,11},{10,... | collective-permute-start | bytes 24584 | tf_op jit(solution)/shard_map/ppermute | solution.py:178
  4.5 2.3 %prepare_sources.1 = (bf16[2,128,1024]{2,1,0:T(8,128)(2,1)S(1)}, f32[2,128,1]{2,1,0:T(8,128)S(1)}, bf16[256,512]{1,0:T(8,128)(2,1)S(1)}) custom-call(s32[1,2]{1,0:T(1,128)} %bitcast.7, s32[2,1,128]{2,1,0:T(1,128)} %order_hbm.1, bf16[2,128,1024]{2,1,0:T(8,128)(2,1)} %bitcast.6, bf16[1,129]{1,0:T(2,128)(2,1)S(1)} %reshape.3.taps_ref), custom_call_target="tpu_custom_call" | custom-call | flops 335544320 | bytes 1048576 | tf_op jit(solution)/shard_map/prepare_sources/pallas_call | solution.py:99
  6.8 0.0 collective-permute-done.1
  6.8 2.7 %collective-permute-start.6 = (bf16[4,2,1024]{2,1,0:T(2,128)(2,1)S(1)}, bf16[4,2,1024]{2,1,0:T(2,128)(2,1)S(1)}, u32[]{:S(2)}, u32[]{:S(2)}) collective-permute-start(bf16[4,2,1024]{2,1,0:T(2,128)(2,1)S(1)} %pad_maximum_fusion.rec_ref), channel_id=1, source_target_pairs={{8,0},{12,4},{0,8},{4,12},{9,1},{13,5},{1,9},{5,13},{10,2},{14,6},... | collective-permute-start | bytes 49160 | tf_op jit(solution)/shard_map/ppermute | solution.py:206
  9.5 1.3 %collective-permute-start.4 = (bf16[4,2,1024]{2,1,0:T(2,128)(2,1)S(1)}, bf16[4,2,1024]{2,1,0:T(2,128)(2,1)S(1)}, u32[]{:S(2)}, u32[]{:S(2)}) collective-permute-start(bf16[4,2,1024]{2,1,0:T(2,128)(2,1)S(1)} %pad_maximum_fusion.rec_ref), channel_id=1, source_target_pairs={{12,0},{8,4},{4,8},{0,12},{13,1},{9,5},{5,9},{1,13},{14,2},{10,6},... | collective-permute-start | bytes 49160 | tf_op jit(solution)/shard_map/ppermute | solution.py:206
  10.8 0.2 collective-permute-start.2
  11.1 0.6 %collective-permute-done.6.rec_ref = bf16[4,2,1024]{2,1,0:T(2,128)(2,1)S(1)} collective-permute-done((bf16[4,2,1024]{2,1,0:T(2,128)(2,1)S(1)}, bf16[4,2,1024]{2,1,0:T(2,128)(2,1)S(1)}, u32[]{:S(2)}, u32[]{:S(2)}) %collective-permute-start.6) | collective-permute-done | bytes 16416 | tf_op jit(solution)/shard_map/ppermute | solution.py:206
  11.6 0.9 %pair_terms.7 = bf16[128,256]{1,0:T(8,128)(2,1)S(1)} custom-call(bf16[4,2,1024]{2,1,0:T(2,128)(2,1)S(1)} %collective-permute-done.6.rec_ref, bf16[256,512]{1,0:T(8,128)(2,1)S(1)} %get-tuple-element.16.band_ref, bf16[2,128,1024]{2,1,0:T(8,128)(2,1)S(1)} %get-tuple-element.17.kept_ref, f32[2,128,1]{2,1,0:T(8,128)S(1)} %get-tuple-element.18.energy_ref), custom_call_target="tpu_custom_call" | custom-call | flops 134217728 | bytes 1048576 | tf_op jit(solution)/shard_map/pair_terms/pallas_call | solution.py:156
  12.5 2.7 %collective-permute-start.7 = (bf16[128,256]{1,0:T(8,128)(2,1)S(1)}, bf16[128,256]{1,0:T(8,128)(2,1)S(1)}, u32[]{:S(2)}, u32[]{:S(2)}) collective-permute-start(bf16[128,256]{1,0:T(8,128)(2,1)S(1)} %pair_terms.7), channel_id=1, source_target_pairs={{0,8},{4,12},{8,0},{12,4},{1,9},{5,13},{9,1},{13,5},{2,10},{6,14},... | collective-permute-start | bytes 196616 | tf_op jit(solution)/shard_map/ppermute | solution.py:210
  15.3 0.0 collective-permute-done.4.rec_ref
  15.3 0.9 %pair_terms.6 = bf16[128,256]{1,0:T(8,128)(2,1)S(1)} custom-call(bf16[4,2,1024]{2,1,0:T(2,128)(2,1)S(1)} %collective-permute-done.4.rec_ref, bf16[256,512]{1,0:T(8,128)(2,1)S(1)} %get-tuple-element.16.band_ref, bf16[2,128,1024]{2,1,0:T(8,128)(2,1)S(1)} %get-tuple-element.17.kept_ref, f32[2,128,1]{2,1,0:T(8,128)S(1)} %get-tuple-element.18.energy_ref), custom_call_target="tpu_custom_call" | custom-call | flops 134217728 | bytes 1048576 | tf_op jit(solution)/shard_map/pair_terms/pallas_call | solution.py:156
  16.1 1.2 %collective-permute-start.5 = (bf16[128,256]{1,0:T(8,128)(2,1)S(1)}, bf16[128,256]{1,0:T(8,128)(2,1)S(1)}, u32[]{:S(2)}, u32[]{:S(2)}) collective-permute-start(bf16[128,256]{1,0:T(8,128)(2,1)S(1)} %pair_terms.6), channel_id=1, source_target_pairs={{0,12},{4,8},{8,4},{12,0},{1,13},{5,9},{9,5},{13,1},{2,14},{6,10},... | collective-permute-start | bytes 196616 | tf_op jit(solution)/shard_map/ppermute | solution.py:210
  17.4 0.0 collective-permute-done.2.rec_ref
  17.4 0.9 %pair_terms.5 = bf16[128,256]{1,0:T(8,128)(2,1)S(1)} custom-call(bf16[4,2,1024]{2,1,0:T(2,128)(2,1)S(1)} %collective-permute-done.2.rec_ref, bf16[256,512]{1,0:T(8,128)(2,1)S(1)} %get-tuple-element.16.band_ref, bf16[2,128,1024]{2,1,0:T(8,128)(2,1)S(1)} %get-tuple-element.17.kept_ref, f32[2,128,1]{2,1,0:T(8,128)S(1)} %get-tuple-element.18.energy_ref), custom_call_target="tpu_custom_call" | custom-call | flops 134217728 | bytes 1048576 | tf_op jit(solution)/shard_map/pair_terms/pallas_call | solution.py:156
  18.3 0.0 copy-start
  18.3 0.6 %collective-permute-start.3 = (bf16[128,256]{1,0:T(8,128)(2,1)S(1)}, bf16[128,256]{1,0:T(8,128)(2,1)S(1)}, u32[]{:S(2)}, u32[]{:S(2)}) collective-permute-start(bf16[128,256]{1,0:T(8,128)(2,1)S(1)} %pair_terms.5), channel_id=1, source_target_pairs={{0,4},{4,0},{8,12},{12,8},{1,5},{5,1},{9,13},{13,9},{2,6},{6,2},{1... | collective-permute-start | bytes 196616 | tf_op jit(solution)/shard_map/ppermute | solution.py:210
  18.8 0.9 %pair_terms.4 = f32[128,256]{1,0:T(8,128)S(1)} custom-call(bf16[4,2,1024]{2,1,0:T(2,128)(2,1)S(1)} %pad_maximum_fusion.rec_ref, bf16[256,512]{1,0:T(8,128)(2,1)S(1)} %get-tuple-element.16.band_ref, bf16[2,128,1024]{2,1,0:T(8,128)(2,1)S(1)} %get-tuple-element.17.kept_ref, f32[2,128,1]{2,1,0:T(8,128)S(1)} %get-tuple-element.18.energy_ref), custom_call_target="tpu_custom_call" | custom-call | flops 134217728 | bytes 1048576 | tf_op jit(solution)/shard_map/pair_terms/pallas_call | solution.py:156
  19.7 0.0 collective-permute-done.7
  19.7 2.6 %collective-permute-done.5 = bf16[128,256]{1,0:T(8,128)(2,1)S(1)} collective-permute-done((bf16[128,256]{1,0:T(8,128)(2,1)S(1)}, bf16[128,256]{1,0:T(8,128)(2,1)S(1)}, u32[]{:S(2)}, u32[]{:S(2)}) %collective-permute-start.5) | collective-permute-done | bytes 65568 | tf_op jit(solution)/shard_map/ppermute | solution.py:210
  22.3 0.7 %collective-permute-done.3 = bf16[128,256]{1,0:T(8,128)(2,1)S(1)} collective-permute-done((bf16[128,256]{1,0:T(8,128)(2,1)S(1)}, bf16[128,256]{1,0:T(8,128)(2,1)S(1)}, u32[]{:S(2)}, u32[]{:S(2)}) %collective-permute-start.3) | collective-permute-done | bytes 65568 | tf_op jit(solution)/shard_map/ppermute | solution.py:210
  23.0 0.0 copy-done
  23.0 0.7 %convert_add_fusion = f32[128,256]{1,0:T(8,128)} fusion(bf16[128,256]{1,0:T(8,128)(2,1)S(1)} %collective-permute-done.7, bf16[128,256]{1,0:T(8,128)(2,1)S(1)} %collective-permute-done.5, bf16[128,256]{1,0:T(8,128)(2,1)S(1)} %collective-permute-done.3, f32[128,256]{1,0:T(8,128)S(1)} %copy-done, f32[128,256]{1,0:T(8,128)S(1)} %pair_terms.4), kind=kLoop, calls=%fused_computation | loop fusion | flops 229376 | bytes 589824 | tf_op jit(solution)/shard_map/add | solution.py:213
  (5 shorter events, 0.1 us)
Async XLA Ops:
  0.0 1.5 %collective-permute-start = (bf16[1,2,1024]{2,1,0:T(2,128)(2,1)}, bf16[1,2,1024]{2,1,0:T(2,128)(2,1)S(1)}, u32[]{:S(2)}, u32[]{:S(2)}) collective-permute-start(bf16[1,2,1024]{2,1,0:T(2,128)(2,1)} %bitcast.5), channel_id=1, source_target_pairs={{0,1},{1,0},{2,3},{3,2},{4,5},{5,4},{6,7},{7,6},{8,9},{9,8},{10,11... | collective-permute-start | bytes 12296 | tf_op jit(solution)/shard_map/ppermute | solution.py:178
  0.5 0.7 %copy-start.2 = (bf16[129]{0:T(256)(128)(2,1)S(1)}, bf16[129]{0:T(256)(128)(2,1)}, u32[]{:S(2)}) copy-start(bf16[129]{0:T(256)(128)(2,1)} %param.10) | copy-start | bytes 778
  0.5 1.0 %copy-start.1 = (bf16[2,1,1024]{2,0,1:T(2,128)(2,1)S(1)}, bf16[2,1,1024]{2,0,1:T(2,128)(2,1)}, u32[]{:S(2)}) copy-start(bf16[2,1,1024]{2,0,1:T(2,128)(2,1)} %param.9) | copy-start | bytes 12292
  1.6 5.2 %collective-permute-start.1 = (bf16[2,2,1024]{2,1,0:T(2,128)(2,1)S(1)}, bf16[2,2,1024]{2,1,0:T(2,128)(2,1)S(1)}, u32[]{:S(2)}, u32[]{:S(2)}) collective-permute-start(bf16[2,2,1024]{2,1,0:T(2,128)(2,1)S(1)} %pad_maximum_fusion.1), channel_id=1, source_target_pairs={{0,2},{1,3},{2,0},{3,1},{4,6},{5,7},{6,4},{7,5},{8,10},{9,11},{10,... | collective-permute-start | bytes 24584 | tf_op jit(solution)/shard_map/ppermute | solution.py:178
  6.8 4.8 %collective-permute-start.6 = (bf16[4,2,1024]{2,1,0:T(2,128)(2,1)S(1)}, bf16[4,2,1024]{2,1,0:T(2,128)(2,1)S(1)}, u32[]{:S(2)}, u32[]{:S(2)}) collective-permute-start(bf16[4,2,1024]{2,1,0:T(2,128)(2,1)S(1)} %pad_maximum_fusion.rec_ref), channel_id=1, source_target_pairs={{8,0},{12,4},{0,8},{4,12},{9,1},{13,5},{1,9},{5,13},{10,2},{14,6},... | collective-permute-start | bytes 49160 | tf_op jit(solution)/shard_map/ppermute | solution.py:206
  9.5 5.8 %collective-permute-start.4 = (bf16[4,2,1024]{2,1,0:T(2,128)(2,1)S(1)}, bf16[4,2,1024]{2,1,0:T(2,128)(2,1)S(1)}, u32[]{:S(2)}, u32[]{:S(2)}) collective-permute-start(bf16[4,2,1024]{2,1,0:T(2,128)(2,1)S(1)} %pad_maximum_fusion.rec_ref), channel_id=1, source_target_pairs={{12,0},{8,4},{4,8},{0,12},{13,1},{9,5},{5,9},{1,13},{14,2},{10,6},... | collective-permute-start | bytes 49160 | tf_op jit(solution)/shard_map/ppermute | solution.py:206
  10.8 6.5 %collective-permute-start.2 = (bf16[4,2,1024]{2,1,0:T(2,128)(2,1)S(1)}, bf16[4,2,1024]{2,1,0:T(2,128)(2,1)S(1)}, u32[]{:S(2)}, u32[]{:S(2)}) collective-permute-start(bf16[4,2,1024]{2,1,0:T(2,128)(2,1)S(1)} %pad_maximum_fusion.rec_ref), channel_id=1, source_target_pairs={{4,0},{0,4},{12,8},{8,12},{5,1},{1,5},{13,9},{9,13},{6,2},{2,6},{1... | collective-permute-start | bytes 49160 | tf_op jit(solution)/shard_map/ppermute | solution.py:206
  12.5 7.2 %collective-permute-start.7 = (bf16[128,256]{1,0:T(8,128)(2,1)S(1)}, bf16[128,256]{1,0:T(8,128)(2,1)S(1)}, u32[]{:S(2)}, u32[]{:S(2)}) collective-permute-start(bf16[128,256]{1,0:T(8,128)(2,1)S(1)} %pair_terms.7), channel_id=1, source_target_pairs={{0,8},{4,12},{8,0},{12,4},{1,9},{5,13},{9,1},{13,5},{2,10},{6,14},... | collective-permute-start | bytes 196616 | tf_op jit(solution)/shard_map/ppermute | solution.py:210
  16.1 6.2 %collective-permute-start.5 = (bf16[128,256]{1,0:T(8,128)(2,1)S(1)}, bf16[128,256]{1,0:T(8,128)(2,1)S(1)}, u32[]{:S(2)}, u32[]{:S(2)}) collective-permute-start(bf16[128,256]{1,0:T(8,128)(2,1)S(1)} %pair_terms.6), channel_id=1, source_target_pairs={{0,12},{4,8},{8,4},{12,0},{1,13},{5,9},{9,5},{13,1},{2,14},{6,10},... | collective-permute-start | bytes 196616 | tf_op jit(solution)/shard_map/ppermute | solution.py:210
  18.3 4.7 %copy-start = (f32[128,256]{1,0:T(8,128)S(1)}, f32[128,256]{1,0:T(8,128)}, u32[]{:S(2)}) copy-start(f32[128,256]{1,0:T(8,128)} %param.11) | copy-start | bytes 393220
  18.3 4.7 %collective-permute-start.3 = (bf16[128,256]{1,0:T(8,128)(2,1)S(1)}, bf16[128,256]{1,0:T(8,128)(2,1)S(1)}, u32[]{:S(2)}, u32[]{:S(2)}) collective-permute-start(bf16[128,256]{1,0:T(8,128)(2,1)S(1)} %pair_terms.5), channel_id=1, source_target_pairs={{0,4},{4,0},{8,12},{12,8},{1,5},{5,1},{9,13},{13,9},{2,6},{6,2},{1... | collective-permute-start | bytes 196616 | tf_op jit(solution)/shard_map/ppermute | solution.py:210

commit v2 on v1

--- a/solution.py
+++ b/solution.py
@@ -173,15 +173,16 @@
     here = lax.axis_index("col")
     if columns & (columns - 1):
         return lax.all_gather(piece, "col", axis=0, tiled=True)
+    found = {0: piece}
+    for step in range(columns - 1, 0, -1):
+        found[step] = lax.ppermute(piece, "col", [(i, i ^ step) for i in range(columns)])
+    pieces = [found[step] for step in range(columns)]
     bit = 1
     while bit < columns:
-        other = lax.ppermute(piece, "col", [(i, i ^ bit) for i in range(columns)])
-        mine_first = (here & bit) == 0
-        piece = jnp.concatenate(
-            [jnp.where(mine_first, piece, other), jnp.where(mine_first, other, piece)], axis=0
-        )
+        flip = (here & bit) != 0
+        pieces = [jnp.where(flip, pieces[i ^ bit], pieces[i]) for i in range(columns)]
         bit *= 2
-    return piece
+    return jnp.concatenate(pieces, axis=0)
 
 
 def shards(mesh_shape, src_raw, block_owner, chan_order, rec_raw, fir_taps, stacks):

time: 23.8 us -> 23.3 us (0.979)
  local copies, waits for them, and re-layouts: 0.67 us -> 0.02 us
  waiting for transfers between devices: 4.21 us -> 4.58 us
    unnamed x6, local copies, waits for them, and re-layouts: 0.66 us -> 0.02 us
    ppermute x2 -> x3, waiting for transfers between devices: 0.38 us -> 0.84 us  [gather_columns(): lax.ppermute(piece, 'col', [(i, i ^ step) for i in range(columns)])]
    ppermute x2 -> x3, starting transfers between devices: 3.38 us -> 3.08 us  [gather_columns(): lax.ppermute(piece, 'col', [(i, i ^ step) for i in range(columns)])]
  transfers between devices with their start and end apart: 8 -> 9, of which waited for: 4 -> 4; matrix products, arithmetic and copies ran while one was open for 0% -> 0% of each run, Pallas kernels for 24% -> 25%
where the time goes in v2:
time: 23.3 us; the launch traced here: 23.1 us
  starting transfers between devices  11.9 us (51%)
  Pallas kernels  5.79 us (25%)
  waiting for transfers between devices  4.58 us (20%)
  other arithmetic  0.74 us (3%)
    ppermute x3, starting transfers between devices, shards(): lax.ppermute(terms(arrived[step], dtype=jnp.bfloat16), 'row', pairs)  4.51 us
    ppermute x3, starting transfers between devices, shards(): arrived[step] = lax.ppermute(receivers, 'row', pairs)  4.3 us
    pallas_call x4, Pallas kernels, pair_terms(): pl.pallas_call(pair_kernel, out_shape=jax.ShapeDtypeStruct((count, receiv...  3.49 us
    ppermute x3, waiting for transfers between devices, shards(): lax.ppermute(terms(arrived[step], dtype=jnp.bfloat16), 'row', pairs)  3.33 us
    ppermute x3, starting transfers between devices, gather_columns(): lax.ppermute(piece, 'col', [(i, i ^ step) for i in range(columns)])  3.08 us
    pallas_call x1, Pallas kernels, prepare_sources(): pl.pallas_call(source_kernel, out_shape=(jax.ShapeDtypeStruct((windows, c...  2.29 us
    ppermute x3, waiting for transfers between devices, gather_columns(): lax.ppermute(piece, 'col', [(i, i ^ step) for i in range(columns)])  0.84 us
    add x1, other arithmetic, shards(): total = total + part.astype(jnp.float32)  0.69 us
  transfers between devices with their start and end apart: 9, of which 4 were waited for; matrix products, arithmetic and copies ran while one was open for 0% of the time, Pallas kernels for 25%

profile of v2, /device:TPU:0, one launch (start us, length us, event | category | flops | bytes accessed | tf_op | source)
XLA Modules:
  0.0 23.1 jit_solution(5065553445434990197)
XLA Ops:
  0.0 0.0 copy-start.2
  0.0 0.5 %collective-permute-start.2 = (bf16[1,2,1024]{2,1,0:T(2,128)(2,1)}, bf16[1,2,1024]{2,1,0:T(2,128)(2,1)S(1)}, u32[]{:S(2)}, u32[]{:S(2)}) collective-permute-start(bf16[1,2,1024]{2,1,0:T(2,128)(2,1)} %bitcast.13), channel_id=1, source_target_pairs={{0,1},{1,0},{2,3},{3,2},{4,5},{5,4},{6,7},{7,6},{8,9},{9,8},{10,11... | collective-permute-start | bytes 12296 | tf_op jit(solution)/shard_map/ppermute | solution.py:178
  0.5 2.5 %collective-permute-start.1 = (bf16[1,2,1024]{2,1,0:T(2,128)(2,1)}, bf16[1,2,1024]{2,1,0:T(2,128)(2,1)S(1)}, u32[]{:S(2)}, u32[]{:S(2)}) collective-permute-start(bf16[1,2,1024]{2,1,0:T(2,128)(2,1)} %bitcast.14), channel_id=1, source_target_pairs={{0,2},{1,3},{2,0},{3,1},{4,6},{5,7},{6,4},{7,5},{8,10},{9,11},{10,... | collective-permute-start | bytes 12296 | tf_op jit(solution)/shard_map/ppermute | solution.py:178
  3.0 0.1 collective-permute-start
  3.1 0.0 copy-done.2
  3.1 2.3 %prepare_sources.1 = (bf16[2,128,1024]{2,1,0:T(8,128)(2,1)S(1)}, f32[2,128,1]{2,1,0:T(8,128)S(1)}, bf16[256,512]{1,0:T(8,128)(2,1)S(1)}) custom-call(s32[1,2]{1,0:T(1,128)} %bitcast.17, s32[2,1,128]{2,1,0:T(1,128)} %order_hbm.1, bf16[2,128,1024]{2,1,0:T(8,128)(2,1)} %bitcast.16, bf16[1,129]{1,0:T(2,128)(2,1)S(1)} %reshape.3.taps_ref), custom_call_target="tpu_custom_call" | custom-call | flops 335544320 | bytes 1048576 | tf_op jit(solution)/shard_map/prepare_sources/pallas_call | solution.py:99
  5.4 0.0 copy-start.1
  5.4 0.0 collective-permute-done.2
  5.4 0.0 collective-permute-done.1
  5.4 0.8 %collective-permute-done = bf16[1,2,1024]{2,1,0:T(2,128)(2,1)S(1)} collective-permute-done((bf16[1,2,1024]{2,1,0:T(2,128)(2,1)}, bf16[1,2,1024]{2,1,0:T(2,128)(2,1)S(1)}, u32[]{:S(2)}, u32[]{:S(2)}) %collective-permute-start) | collective-permute-done | bytes 4128 | tf_op jit(solution)/shard_map/ppermute | solution.py:178
  6.3 0.0 copy-done.1
  6.3 2.7 %collective-permute-start.7 = (bf16[4,2,1024]{2,1,0:T(2,128)(2,1)S(1)}, bf16[4,2,1024]{2,1,0:T(2,128)(2,1)S(1)}, u32[]{:S(2)}, u32[]{:S(2)}) collective-permute-start(bf16[4,2,1024]{2,1,0:T(2,128)(2,1)S(1)} %pad_maximum_fusion.rec_ref), channel_id=1, source_target_pairs={{8,0},{12,4},{0,8},{4,12},{9,1},{13,5},{1,9},{5,13},{10,2},{14,6},... | collective-permute-start | bytes 49160 | tf_op jit(solution)/shard_map/ppermute | solution.py:207
  9.1 1.3 %collective-permute-start.5 = (bf16[4,2,1024]{2,1,0:T(2,128)(2,1)S(1)}, bf16[4,2,1024]{2,1,0:T(2,128)(2,1)S(1)}, u32[]{:S(2)}, u32[]{:S(2)}) collective-permute-start(bf16[4,2,1024]{2,1,0:T(2,128)(2,1)S(1)} %pad_maximum_fusion.rec_ref), channel_id=1, source_target_pairs={{12,0},{8,4},{4,8},{0,12},{13,1},{9,5},{5,9},{1,13},{14,2},{10,6},... | collective-permute-start | bytes 49160 | tf_op jit(solution)/shard_map/ppermute | solution.py:207
  10.4 0.2 %collective-permute-start.3 = (bf16[4,2,1024]{2,1,0:T(2,128)(2,1)S(1)}, bf16[4,2,1024]{2,1,0:T(2,128)(2,1)S(1)}, u32[]{:S(2)}, u32[]{:S(2)}) collective-permute-start(bf16[4,2,1024]{2,1,0:T(2,128)(2,1)S(1)} %pad_maximum_fusion.rec_ref), channel_id=1, source_target_pairs={{4,0},{0,4},{12,8},{8,12},{5,1},{1,5},{13,9},{9,13},{6,2},{2,6},{1... | collective-permute-start | bytes 49160 | tf_op jit(solution)/shard_map/ppermute | solution.py:207
  10.6 0.4 %collective-permute-done.7.rec_ref = bf16[4,2,1024]{2,1,0:T(2,128)(2,1)S(1)} collective-permute-done((bf16[4,2,1024]{2,1,0:T(2,128)(2,1)S(1)}, bf16[4,2,1024]{2,1,0:T(2,128)(2,1)S(1)}, u32[]{:S(2)}, u32[]{:S(2)}) %collective-permute-start.7) | collective-permute-done | bytes 16416 | tf_op jit(solution)/shard_map/ppermute | solution.py:207
  11.0 0.9 %pair_terms.7 = bf16[128,256]{1,0:T(8,128)(2,1)S(1)} custom-call(bf16[4,2,1024]{2,1,0:T(2,128)(2,1)S(1)} %collective-permute-done.7.rec_ref, bf16[256,512]{1,0:T(8,128)(2,1)S(1)} %get-tuple-element.16.band_ref, bf16[2,128,1024]{2,1,0:T(8,128)(2,1)S(1)} %get-tuple-element.17.kept_ref, f32[2,128,1]{2,1,0:T(8,128)S(1)} %get-tuple-element.18.energy_ref), custom_call_target="tpu_custom_call" | custom-call | flops 134217728 | bytes 1048576 | tf_op jit(solution)/shard_map/pair_terms/pallas_call | solution.py:156
  11.9 2.7 %collective-permute-start.8 = (bf16[128,256]{1,0:T(8,128)(2,1)S(1)}, bf16[128,256]{1,0:T(8,128)(2,1)S(1)}, u32[]{:S(2)}, u32[]{:S(2)}) collective-permute-start(bf16[128,256]{1,0:T(8,128)(2,1)S(1)} %pair_terms.7), channel_id=1, source_target_pairs={{0,8},{4,12},{8,0},{12,4},{1,9},{5,13},{9,1},{13,5},{2,10},{6,14},... | collective-permute-start | bytes 196616 | tf_op jit(solution)/shard_map/ppermute | solution.py:211
  14.7 0.0 collective-permute-done.5.rec_ref
  14.7 0.9 %pair_terms.6 = bf16[128,256]{1,0:T(8,128)(2,1)S(1)} custom-call(bf16[4,2,1024]{2,1,0:T(2,128)(2,1)S(1)} %collective-permute-done.5.rec_ref, bf16[256,512]{1,0:T(8,128)(2,1)S(1)} %get-tuple-element.16.band_ref, bf16[2,128,1024]{2,1,0:T(8,128)(2,1)S(1)} %get-tuple-element.17.kept_ref, f32[2,128,1]{2,1,0:T(8,128)S(1)} %get-tuple-element.18.energy_ref), custom_call_target="tpu_custom_call" | custom-call | flops 134217728 | bytes 1048576 | tf_op jit(solution)/shard_map/pair_terms/pallas_call | solution.py:156
  15.5 1.4 %collective-permute-start.6 = (bf16[128,256]{1,0:T(8,128)(2,1)S(1)}, bf16[128,256]{1,0:T(8,128)(2,1)S(1)}, u32[]{:S(2)}, u32[]{:S(2)}) collective-permute-start(bf16[128,256]{1,0:T(8,128)(2,1)S(1)} %pair_terms.6), channel_id=1, source_target_pairs={{0,12},{4,8},{8,4},{12,0},{1,13},{5,9},{9,5},{13,1},{2,14},{6,10},... | collective-permute-start | bytes 196616 | tf_op jit(solution)/shard_map/ppermute | solution.py:211
  16.9 0.0 collective-permute-done.3.rec_ref
  17.0 0.9 %pair_terms.5 = bf16[128,256]{1,0:T(8,128)(2,1)S(1)} custom-call(bf16[4,2,1024]{2,1,0:T(2,128)(2,1)S(1)} %collective-permute-done.3.rec_ref, bf16[256,512]{1,0:T(8,128)(2,1)S(1)} %get-tuple-element.16.band_ref, bf16[2,128,1024]{2,1,0:T(8,128)(2,1)S(1)} %get-tuple-element.17.kept_ref, f32[2,128,1]{2,1,0:T(8,128)S(1)} %get-tuple-element.18.energy_ref), custom_call_target="tpu_custom_call" | custom-call | flops 134217728 | bytes 1048576 | tf_op jit(solution)/shard_map/pair_terms/pallas_call | solution.py:156
  17.8 0.0 copy-start
  17.8 0.4 %collective-permute-start.4 = (bf16[128,256]{1,0:T(8,128)(2,1)S(1)}, bf16[128,256]{1,0:T(8,128)(2,1)S(1)}, u32[]{:S(2)}, u32[]{:S(2)}) collective-permute-start(bf16[128,256]{1,0:T(8,128)(2,1)S(1)} %pair_terms.5), channel_id=1, source_target_pairs={{0,4},{4,0},{8,12},{12,8},{1,5},{5,1},{9,13},{13,9},{2,6},{6,2},{1... | collective-permute-start | bytes 196616 | tf_op jit(solution)/shard_map/ppermute | solution.py:211
  18.2 0.9 %pair_terms.4 = f32[128,256]{1,0:T(8,128)S(1)} custom-call(bf16[4,2,1024]{2,1,0:T(2,128)(2,1)S(1)} %pad_maximum_fusion.rec_ref, bf16[256,512]{1,0:T(8,128)(2,1)S(1)} %get-tuple-element.16.band_ref, bf16[2,128,1024]{2,1,0:T(8,128)(2,1)S(1)} %get-tuple-element.17.kept_ref, f32[2,128,1]{2,1,0:T(8,128)S(1)} %get-tuple-element.18.energy_ref), custom_call_target="tpu_custom_call" | custom-call | flops 134217728 | bytes 1048576 | tf_op jit(solution)/shard_map/pair_terms/pallas_call | solution.py:156
  19.1 0.0 collective-permute-done.8
  19.1 2.6 %collective-permute-done.6 = bf16[128,256]{1,0:T(8,128)(2,1)S(1)} collective-permute-done((bf16[128,256]{1,0:T(8,128)(2,1)S(1)}, bf16[128,256]{1,0:T(8,128)(2,1)S(1)}, u32[]{:S(2)}, u32[]{:S(2)}) %collective-permute-start.6) | collective-permute-done | bytes 65568 | tf_op jit(solution)/shard_map/ppermute | solution.py:211
  21.8 0.7 %collective-permute-done.4 = bf16[128,256]{1,0:T(8,128)(2,1)S(1)} collective-permute-done((bf16[128,256]{1,0:T(8,128)(2,1)S(1)}, bf16[128,256]{1,0:T(8,128)(2,1)S(1)}, u32[]{:S(2)}, u32[]{:S(2)}) %collective-permute-start.4) | collective-permute-done | bytes 65568 | tf_op jit(solution)/shard_map/ppermute | solution.py:211
  22.4 0.0 copy-done
  22.4 0.7 %convert_add_fusion = f32[128,256]{1,0:T(8,128)} fusion(bf16[128,256]{1,0:T(8,128)(2,1)S(1)} %collective-permute-done.8, bf16[128,256]{1,0:T(8,128)(2,1)S(1)} %collective-permute-done.6, bf16[128,256]{1,0:T(8,128)(2,1)S(1)} %collective-permute-done.4, f32[128,256]{1,0:T(8,128)S(1)} %copy-done, f32[128,256]{1,0:T(8,128)S(1)} %pair_terms.4), kind=kLoop, calls=%fused_computation | loop fusion | flops 229376 | bytes 589824 | tf_op jit(solution)/shard_map/add | solution.py:214
  (3 shorter events, 0.1 us)
Async XLA Ops:
  0.0 3.1 %copy-start.2 = (bf16[129]{0:T(256)(128)(2,1)S(1)}, bf16[129]{0:T(256)(128)(2,1)}, u32[]{:S(2)}) copy-start(bf16[129]{0:T(256)(128)(2,1)} %param.10) | copy-start | bytes 778
  0.0 5.4 %collective-permute-start.2 = (bf16[1,2,1024]{2,1,0:T(2,128)(2,1)}, bf16[1,2,1024]{2,1,0:T(2,128)(2,1)S(1)}, u32[]{:S(2)}, u32[]{:S(2)}) collective-permute-start(bf16[1,2,1024]{2,1,0:T(2,128)(2,1)} %bitcast.13), channel_id=1, source_target_pairs={{0,1},{1,0},{2,3},{3,2},{4,5},{5,4},{6,7},{7,6},{8,9},{9,8},{10,11... | collective-permute-start | bytes 12296 | tf_op jit(solution)/shard_map/ppermute | solution.py:178
  0.5 4.9 %collective-permute-start.1 = (bf16[1,2,1024]{2,1,0:T(2,128)(2,1)}, bf16[1,2,1024]{2,1,0:T(2,128)(2,1)S(1)}, u32[]{:S(2)}, u32[]{:S(2)}) collective-permute-start(bf16[1,2,1024]{2,1,0:T(2,128)(2,1)} %bitcast.14), channel_id=1, source_target_pairs={{0,2},{1,3},{2,0},{3,1},{4,6},{5,7},{6,4},{7,5},{8,10},{9,11},{10,... | collective-permute-start | bytes 12296 | tf_op jit(solution)/shard_map/ppermute | solution.py:178
  3.0 3.2 %collective-permute-start = (bf16[1,2,1024]{2,1,0:T(2,128)(2,1)}, bf16[1,2,1024]{2,1,0:T(2,128)(2,1)S(1)}, u32[]{:S(2)}, u32[]{:S(2)}) collective-permute-start(bf16[1,2,1024]{2,1,0:T(2,128)(2,1)} %bitcast.15), channel_id=1, source_target_pairs={{0,3},{1,2},{2,1},{3,0},{4,7},{5,6},{6,5},{7,4},{8,11},{9,10},{10,... | collective-permute-start | bytes 12296 | tf_op jit(solution)/shard_map/ppermute | solution.py:178
  5.4 0.9 %copy-start.1 = (bf16[2,1,1024]{2,0,1:T(2,128)(2,1)S(1)}, bf16[2,1,1024]{2,0,1:T(2,128)(2,1)}, u32[]{:S(2)}) copy-start(bf16[2,1,1024]{2,0,1:T(2,128)(2,1)} %param.9) | copy-start | bytes 12292
  6.3 4.7 %collective-permute-start.7 = (bf16[4,2,1024]{2,1,0:T(2,128)(2,1)S(1)}, bf16[4,2,1024]{2,1,0:T(2,128)(2,1)S(1)}, u32[]{:S(2)}, u32[]{:S(2)}) collective-permute-start(bf16[4,2,1024]{2,1,0:T(2,128)(2,1)S(1)} %pad_maximum_fusion.rec_ref), channel_id=1, source_target_pairs={{8,0},{12,4},{0,8},{4,12},{9,1},{13,5},{1,9},{5,13},{10,2},{14,6},... | collective-permute-start | bytes 49160 | tf_op jit(solution)/shard_map/ppermute | solution.py:207
  9.1 5.6 %collective-permute-start.5 = (bf16[4,2,1024]{2,1,0:T(2,128)(2,1)S(1)}, bf16[4,2,1024]{2,1,0:T(2,128)(2,1)S(1)}, u32[]{:S(2)}, u32[]{:S(2)}) collective-permute-start(bf16[4,2,1024]{2,1,0:T(2,128)(2,1)S(1)} %pad_maximum_fusion.rec_ref), channel_id=1, source_target_pairs={{12,0},{8,4},{4,8},{0,12},{13,1},{9,5},{5,9},{1,13},{14,2},{10,6},... | collective-permute-start | bytes 49160 | tf_op jit(solution)/shard_map/ppermute | solution.py:207
  10.4 6.5 %collective-permute-start.3 = (bf16[4,2,1024]{2,1,0:T(2,128)(2,1)S(1)}, bf16[4,2,1024]{2,1,0:T(2,128)(2,1)S(1)}, u32[]{:S(2)}, u32[]{:S(2)}) collective-permute-start(bf16[4,2,1024]{2,1,0:T(2,128)(2,1)S(1)} %pad_maximum_fusion.rec_ref), channel_id=1, source_target_pairs={{4,0},{0,4},{12,8},{8,12},{5,1},{1,5},{13,9},{9,13},{6,2},{2,6},{1... | collective-permute-start | bytes 49160 | tf_op jit(solution)/shard_map/ppermute | solution.py:207
  11.9 7.2 %collective-permute-start.8 = (bf16[128,256]{1,0:T(8,128)(2,1)S(1)}, bf16[128,256]{1,0:T(8,128)(2,1)S(1)}, u32[]{:S(2)}, u32[]{:S(2)}) collective-permute-start(bf16[128,256]{1,0:T(8,128)(2,1)S(1)} %pair_terms.7), channel_id=1, source_target_pairs={{0,8},{4,12},{8,0},{12,4},{1,9},{5,13},{9,1},{13,5},{2,10},{6,14},... | collective-permute-start | bytes 196616 | tf_op jit(solution)/shard_map/ppermute | solution.py:211
  15.5 6.2 %collective-permute-start.6 = (bf16[128,256]{1,0:T(8,128)(2,1)S(1)}, bf16[128,256]{1,0:T(8,128)(2,1)S(1)}, u32[]{:S(2)}, u32[]{:S(2)}) collective-permute-start(bf16[128,256]{1,0:T(8,128)(2,1)S(1)} %pair_terms.6), channel_id=1, source_target_pairs={{0,12},{4,8},{8,4},{12,0},{1,13},{5,9},{9,5},{13,1},{2,14},{6,10},... | collective-permute-start | bytes 196616 | tf_op jit(solution)/shard_map/ppermute | solution.py:211
  17.8 4.6 %copy-start = (f32[128,256]{1,0:T(8,128)S(1)}, f32[128,256]{1,0:T(8,128)}, u32[]{:S(2)}) copy-start(f32[128,256]{1,0:T(8,128)} %param.11) | copy-start | bytes 393220
  17.8 4.6 %collective-permute-start.4 = (bf16[128,256]{1,0:T(8,128)(2,1)S(1)}, bf16[128,256]{1,0:T(8,128)(2,1)S(1)}, u32[]{:S(2)}, u32[]{:S(2)}) collective-permute-start(bf16[128,256]{1,0:T(8,128)(2,1)S(1)} %pair_terms.5), channel_id=1, source_target_pairs={{0,4},{4,0},{8,12},{12,8},{1,5},{5,1},{9,13},{13,9},{2,6},{6,2},{1... | collective-permute-start | bytes 196616 | tf_op jit(solution)/shard_map/ppermute | solution.py:211

commit v3 on v2

--- a/solution.py
+++ b/solution.py
@@ -45,6 +45,7 @@
     kept_ref,
     energy_ref,
     band_ref,
+    mine_ref,
     owner_ref,
     order_ref,
     raw_ref,
@@ -79,6 +80,8 @@
     here = lax.axis_index("row")
     owner_copy.wait()
     order_copy.wait()
+    mine = sum(jnp.where(owner_ref[0, window] == here, 1 << window, 0) for window in range(windows))
+    mine_ref[...] = jnp.full(mine_ref.shape, mine, jnp.int32)
     for window in range(windows):
         place = lax.broadcasted_iota(jnp.int32, (count, count), 0)
         order = jnp.where(owner_ref[0, window] == here, order_ref[window], -1)
@@ -102,9 +105,10 @@
             jax.ShapeDtypeStruct((windows, count, length), jnp.bfloat16),
             jax.ShapeDtypeStruct((windows, count, 1), jnp.float32),
             jax.ShapeDtypeStruct((block, width), jnp.bfloat16),
+            jax.ShapeDtypeStruct((1, LANES), jnp.int32),
         ),
         in_specs=[HBM, HBM, HBM, VMEM],
-        out_specs=(VMEM, VMEM, VMEM),
+        out_specs=(VMEM, VMEM, VMEM, VMEM),
         scratch_shapes=[
             pltpu.SMEM((1, windows), jnp.int32),
             pltpu.VMEM((windows, 1, count), jnp.int32),
@@ -122,43 +126,79 @@
     )(in_hbm(block_owner.T), in_hbm(chan_order), in_hbm(raw), fir_taps.reshape(1, taps))
 
 
-def pair_kernel(rec_ref, band_ref, kept_ref, energy_ref, out_ref, hankel_ref):
-    receivers, windows, length = rec_ref.shape
-    rows = receivers * windows
-    raw = jnp.concatenate([rec_ref[q].astype(jnp.float32) for q in range(receivers)], axis=0)
-    rec = filter_rows(raw, band_ref[...])
+def window_terms(windows, rec_ref, band_ref, kept_ref, energy_ref, hankel_ref):
+    receivers, _, length = rec_ref.shape
+    count = len(windows)
+    rows = receivers * count
+    raw = [rec_ref[q, windows[0] : windows[0] + count].astype(jnp.float32) for q in range(receivers)]
+    rec = filter_rows(jnp.concatenate(raw, axis=0), band_ref[...])
     rec = rec.astype(jnp.bfloat16).astype(jnp.float32)
     rec_energy = jnp.sum(jnp.square(rec), axis=1, keepdims=True)
     padded = jnp.concatenate([rec, jnp.zeros((rows, LANES), jnp.float32)], axis=1)
     width = length + LANES
-    for window in range(windows):
+    for i in range(count):
         for q in range(receivers):
-            at = q * windows + window
+            at = q * count + i
             spread = jnp.broadcast_to(padded[at : at + 1], (LAGS, width))
             shifted = pltpu.roll(spread, width - LAGS // 2, 1, stride=1, stride_axis=0)
-            hankel_ref[window, q * LAGS : (q + 1) * LAGS] = shifted[:, :length].astype(jnp.bfloat16)
+            hankel_ref[windows[i], q * LAGS : (q + 1) * LAGS] = shifted[:, :length].astype(jnp.bfloat16)
     lane = lax.broadcasted_iota(jnp.int32, (rows, receivers * LAGS), 1) // LAGS
     row = lax.broadcasted_iota(jnp.int32, (rows, receivers * LAGS), 0)
     total = None
-    for window in range(windows):
-        own = jnp.where(row == lane * windows + window, rec_energy, 0.0)
+    for i, window in enumerate(windows):
+        own = jnp.where(row == lane * count + i, rec_energy, 0.0)
         across = jnp.sum(own, axis=0, keepdims=True)
         lagged = dot_nt(kept_ref[window], hankel_ref[window])
         ratio = lagged * lax.rsqrt(energy_ref[window] * across + 1e-06)
         term = jnp.tanh(0.5 * math.sqrt(length) * ratio)
         total = term if total is None else total + term
-    out_ref[...] = total.astype(out_ref.dtype)
-
-
-def pair_terms(rec, band, kept, energy, dtype):
+    return total
+
+
+def pair_kernel(rec_ref, band_ref, kept_ref, energy_ref, mine_ref, out_ref, hankel_ref, total_ref):
+    windows = kept_ref.shape[0]
+    terms = functools.partial(
+        window_terms,
+        rec_ref=rec_ref,
+        band_ref=band_ref,
+        kept_ref=kept_ref,
+        energy_ref=energy_ref,
+        hankel_ref=hankel_ref,
+    )
+    mine = mine_ref[0:1, 0:1][0, 0]
+    every = (1 << windows) - 1
+
+    @pl.when(mine == every)
+    def _():
+        out_ref[...] = terms(range(windows)).astype(out_ref.dtype)
+
+    @pl.when(mine != every)
+    def _():
+        total_ref[...] = jnp.zeros_like(total_ref)
+
+    for window in range(windows):
+
+        @pl.when((mine != every) & ((mine >> window) & 1 == 1))
+        def _():
+            total_ref[...] += terms(range(window, window + 1))
+
+    @pl.when(mine != every)
+    def _():
+        out_ref[...] = total_ref[...].astype(out_ref.dtype)
+
+
+def pair_terms(rec, band, kept, energy, mine, dtype):
     receivers, windows, length = rec.shape
     count = kept.shape[1]
     return pl.pallas_call(
         pair_kernel,
         out_shape=jax.ShapeDtypeStruct((count, receivers * LAGS), dtype),
-        in_specs=[VMEM] * 4,
+        in_specs=[VMEM] * 5,
         out_specs=VMEM,
-        scratch_shapes=[pltpu.VMEM((windows, receivers * LAGS, length), jnp.bfloat16)],
+        scratch_shapes=[
+            pltpu.VMEM((windows, receivers * LAGS, length), jnp.bfloat16),
+            pltpu.VMEM((count, receivers * LAGS), jnp.float32),
+        ],
         cost_estimate=pl.CostEstimate(
             flops=2 * windows * count * length * receivers * LAGS,
             bytes_accessed=4 * windows * count * length,
@@ -166,7 +206,7 @@
         ),
         compiler_params=pltpu.CompilerParams(vmem_limit_bytes=VMEM_GRANT),
         name="pair_terms",
-    )(rec, band, kept, energy)
+    )(rec, band, kept, energy, mine)
 
 
 def gather_columns(piece, columns):
@@ -187,10 +227,11 @@
 
 def shards(mesh_shape, src_raw, block_owner, chan_order, rec_raw, fir_taps, stacks):
     rows, columns = mesh_shape["row"], mesh_shape["col"]
-    kept, energy, band = prepare_sources(block_owner, chan_order, src_raw[0], fir_taps)
+    prepared = prepare_sources(block_owner, chan_order, src_raw[0], fir_taps)
     receivers = gather_columns(jnp.swapaxes(rec_raw, 0, 1), columns)
-    receivers, kept, energy, band = lax.optimization_barrier((receivers, kept, energy, band))
-    terms = functools.partial(pair_terms, band=band, kept=kept, energy=energy)
+    receivers, prepared = lax.optimization_barrier((receivers, prepared))
+    kept, energy, band, mine = prepared
+    terms = functools.partial(pair_terms, band=band, kept=kept, energy=energy, mine=mine)
     if rows > DIRECT_ROWS:
         everyone = lax.all_gather(receivers, "row", axis=0)
         parts = lax.map(lambda rec: terms(rec, dtype=jnp.bfloat16), everyone)

time: 23.3 us -> 22.9 us (0.983)
  waiting for transfers between devices: 4.58 us -> 5.77 us
  starting transfers between devices: 11.9 us -> 10.9 us
  Pallas kernels: 5.79 us -> 5.36 us
    ppermute x3, starting transfers between devices: 4.51 us -> 3.51 us  [shards(): lax.ppermute(terms(arrived[step], dtype=jnp.bfloat16), 'row', pairs)]
    ppermute x3, waiting for transfers between devices: 0.41 us -> 1.16 us  [shards(): arrived[step] = lax.ppermute(receivers, 'row', pairs)]
    ppermute x3, waiting for transfers between devices: 3.33 us -> 3.76 us  [shards(): lax.ppermute(terms(arrived[step], dtype=jnp.bfloat16), 'row', pairs)]
    pallas_call x4, Pallas kernels: 3.49 us -> 3.06 us  [pair_terms(): pl.pallas_call(pair_kernel, out_shape=jax.ShapeDtypeStruct((count, receiv...]
  transfers between devices with their start and end apart: 9 -> 9, of which waited for: 4 -> 5; matrix products, arithmetic and copies ran while one was open for 0% -> 0% of each run, Pallas kernels for 25% -> 23%
where the time goes in v3:
time: 22.9 us
  starting transfers between devices  10.9 us (48%)
  waiting for transfers between devices  5.77 us (25%)
  Pallas kernels  5.36 us (23%)
  other arithmetic  0.74 us (3%)
    ppermute x3, starting transfers between devices, shards(): arrived[step] = lax.ppermute(receivers, 'row', pairs)  4.3 us
    ppermute x3, waiting for transfers between devices, shards(): lax.ppermute(terms(arrived[step], dtype=jnp.bfloat16), 'row', pairs)  3.76 us
    ppermute x3, starting transfers between devices, shards(): lax.ppermute(terms(arrived[step], dtype=jnp.bfloat16), 'row', pairs)  3.51 us
    ppermute x3, starting transfers between devices, gather_columns(): lax.ppermute(piece, 'col', [(i, i ^ step) for i in range(columns)])  3.08 us
    pallas_call x4, Pallas kernels, pair_terms(): pl.pallas_call(pair_kernel, out_shape=jax.ShapeDtypeStruct((count, receiv...  3.06 us
    pallas_call x1, Pallas kernels, prepare_sources(): pl.pallas_call(source_kernel, out_shape=(jax.ShapeDtypeStruct((windows, c...  2.29 us
    ppermute x3, waiting for transfers between devices, shards(): arrived[step] = lax.ppermute(receivers, 'row', pairs)  1.16 us
    ppermute x3, waiting for transfers between devices, gather_columns(): lax.ppermute(piece, 'col', [(i, i ^ step) for i in range(columns)])  0.84 us
  transfers between devices with their start and end apart: 9, of which 5 were waited for; matrix products, arithmetic and copies ran while one was open for 0% of the time, Pallas kernels for 23%

profile of v3, /device:TPU:0, one launch (start us, length us, event | category | flops | bytes accessed | tf_op | source)
XLA Modules:
  0.0 22.9 jit_solution(8821286253981459754)
XLA Ops:
  0.0 0.0 copy-start.2
  0.0 0.5 %collective-permute-start.2 = (bf16[1,2,1024]{2,1,0:T(2,128)(2,1)}, bf16[1,2,1024]{2,1,0:T(2,128)(2,1)S(1)}, u32[]{:S(2)}, u32[]{:S(2)}) collective-permute-start(bf16[1,2,1024]{2,1,0:T(2,128)(2,1)} %bitcast.13), channel_id=1, source_target_pairs={{0,1},{1,0},{2,3},{3,2},{4,5},{5,4},{6,7},{7,6},{8,9},{9,8},{10,11... | collective-permute-start | bytes 12296 | tf_op jit(solution)/shard_map/ppermute | solution.py:218
  0.5 2.5 %collective-permute-start.1 = (bf16[1,2,1024]{2,1,0:T(2,128)(2,1)}, bf16[1,2,1024]{2,1,0:T(2,128)(2,1)S(1)}, u32[]{:S(2)}, u32[]{:S(2)}) collective-permute-start(bf16[1,2,1024]{2,1,0:T(2,128)(2,1)} %bitcast.14), channel_id=1, source_target_pairs={{0,2},{1,3},{2,0},{3,1},{4,6},{5,7},{6,4},{7,5},{8,10},{9,11},{10,... | collective-permute-start | bytes 12296 | tf_op jit(solution)/shard_map/ppermute | solution.py:218
  3.0 0.1 collective-permute-start
  3.1 0.0 copy-done.2
  3.1 2.3 %prepare_sources.1 = (bf16[2,128,1024]{2,1,0:T(8,128)(2,1)S(1)}, f32[2,128,1]{2,1,0:T(8,128)S(1)}, bf16[256,512]{1,0:T(8,128)(2,1)S(1)}, s32[1,128]{1,0:T(1,128)S(1)}) custom-call(s32[1,2]{1,0:T(1,128)} %bitcast.17, s32[2,1,128]{2,1,0:T(1,128)} %order_hbm.1, bf16[2,128,1024]{2,1,0:T(8,128)(2,1)} %bitcast.16, bf16[1,129]{1,0:T(2,128)(2,1)S(1)} %reshape.3.taps_ref), custom_call_target="tpu_custom_call" | custom-call | flops 335544320 | bytes 1048576 | tf_op jit(solution)/shard_map/prepare_sources/pallas_call | solution.py:102
  5.4 0.0 copy-start.1
  5.4 0.0 collective-permute-done.2
  5.4 0.0 collective-permute-done.1
  5.4 0.8 %collective-permute-done = bf16[1,2,1024]{2,1,0:T(2,128)(2,1)S(1)} collective-permute-done((bf16[1,2,1024]{2,1,0:T(2,128)(2,1)}, bf16[1,2,1024]{2,1,0:T(2,128)(2,1)S(1)}, u32[]{:S(2)}, u32[]{:S(2)}) %collective-permute-start) | collective-permute-done | bytes 4128 | tf_op jit(solution)/shard_map/ppermute | solution.py:218
  6.3 0.0 copy-done.1
  6.3 2.7 %collective-permute-start.7 = (bf16[4,2,1024]{2,1,0:T(2,128)(2,1)S(1)}, bf16[4,2,1024]{2,1,0:T(2,128)(2,1)S(1)}, u32[]{:S(2)}, u32[]{:S(2)}) collective-permute-start(bf16[4,2,1024]{2,1,0:T(2,128)(2,1)S(1)} %pad_maximum_fusion.rec_ref), channel_id=1, source_target_pairs={{8,0},{12,4},{0,8},{4,12},{9,1},{13,5},{1,9},{5,13},{10,2},{14,6},... | collective-permute-start | bytes 49160 | tf_op jit(solution)/shard_map/ppermute | solution.py:248
  9.1 1.3 %collective-permute-start.5 = (bf16[4,2,1024]{2,1,0:T(2,128)(2,1)S(1)}, bf16[4,2,1024]{2,1,0:T(2,128)(2,1)S(1)}, u32[]{:S(2)}, u32[]{:S(2)}) collective-permute-start(bf16[4,2,1024]{2,1,0:T(2,128)(2,1)S(1)} %pad_maximum_fusion.rec_ref), channel_id=1, source_target_pairs={{12,0},{8,4},{4,8},{0,12},{13,1},{9,5},{5,9},{1,13},{14,2},{10,6},... | collective-permute-start | bytes 49160 | tf_op jit(solution)/shard_map/ppermute | solution.py:248
  10.4 0.2 %collective-permute-start.3 = (bf16[4,2,1024]{2,1,0:T(2,128)(2,1)S(1)}, bf16[4,2,1024]{2,1,0:T(2,128)(2,1)S(1)}, u32[]{:S(2)}, u32[]{:S(2)}) collective-permute-start(bf16[4,2,1024]{2,1,0:T(2,128)(2,1)S(1)} %pad_maximum_fusion.rec_ref), channel_id=1, source_target_pairs={{4,0},{0,4},{12,8},{8,12},{5,1},{1,5},{13,9},{9,13},{6,2},{2,6},{1... | collective-permute-start | bytes 49160 | tf_op jit(solution)/shard_map/ppermute | solution.py:248
  10.6 0.4 %collective-permute-done.7.rec_ref = bf16[4,2,1024]{2,1,0:T(2,128)(2,1)S(1)} collective-permute-done((bf16[4,2,1024]{2,1,0:T(2,128)(2,1)S(1)}, bf16[4,2,1024]{2,1,0:T(2,128)(2,1)S(1)}, u32[]{:S(2)}, u32[]{:S(2)}) %collective-permute-start.7) | collective-permute-done | bytes 16416 | tf_op jit(solution)/shard_map/ppermute | solution.py:248
  11.0 0.8 %pair_terms.7 = bf16[128,256]{1,0:T(8,128)(2,1)S(1)} custom-call(bf16[4,2,1024]{2,1,0:T(2,128)(2,1)S(1)} %collective-permute-done.7.rec_ref, bf16[256,512]{1,0:T(8,128)(2,1)S(1)} %get-tuple-element.19.band_ref, bf16[2,128,1024]{2,1,0:T(8,128)(2,1)S(1)} %get-tuple-element.20.kept_ref, f32[2,128,1]{2,1,0:T(8,128)S(1)} %get-tuple-element.21.energy_ref, ...), custom_call_target="tpu_custom_call" | custom-call | flops 134217728 | bytes 1048576 | tf_op jit(solution)/shard_map/pair_terms/pallas_call | solution.py:193
  11.8 2.0 %collective-permute-start.8 = (bf16[128,256]{1,0:T(8,128)(2,1)S(1)}, bf16[128,256]{1,0:T(8,128)(2,1)S(1)}, u32[]{:S(2)}, u32[]{:S(2)}) collective-permute-start(bf16[128,256]{1,0:T(8,128)(2,1)S(1)} %pair_terms.7), channel_id=1, source_target_pairs={{0,8},{4,12},{8,0},{12,4},{1,9},{5,13},{9,1},{13,5},{2,10},{6,14},... | collective-permute-start | bytes 196616 | tf_op jit(solution)/shard_map/ppermute | solution.py:252
  13.8 0.8 %collective-permute-done.5.rec_ref = bf16[4,2,1024]{2,1,0:T(2,128)(2,1)S(1)} collective-permute-done((bf16[4,2,1024]{2,1,0:T(2,128)(2,1)S(1)}, bf16[4,2,1024]{2,1,0:T(2,128)(2,1)S(1)}, u32[]{:S(2)}, u32[]{:S(2)}) %collective-permute-start.5) | collective-permute-done | bytes 16416 | tf_op jit(solution)/shard_map/ppermute | solution.py:248
  14.6 0.8 %pair_terms.6 = bf16[128,256]{1,0:T(8,128)(2,1)S(1)} custom-call(bf16[4,2,1024]{2,1,0:T(2,128)(2,1)S(1)} %collective-permute-done.5.rec_ref, bf16[256,512]{1,0:T(8,128)(2,1)S(1)} %get-tuple-element.19.band_ref, bf16[2,128,1024]{2,1,0:T(8,128)(2,1)S(1)} %get-tuple-element.20.kept_ref, f32[2,128,1]{2,1,0:T(8,128)S(1)} %get-tuple-element.21.energy_ref, ...), custom_call_target="tpu_custom_call" | custom-call | flops 134217728 | bytes 1048576 | tf_op jit(solution)/shard_map/pair_terms/pallas_call | solution.py:193
  15.4 1.4 %collective-permute-start.6 = (bf16[128,256]{1,0:T(8,128)(2,1)S(1)}, bf16[128,256]{1,0:T(8,128)(2,1)S(1)}, u32[]{:S(2)}, u32[]{:S(2)}) collective-permute-start(bf16[128,256]{1,0:T(8,128)(2,1)S(1)} %pair_terms.6), channel_id=1, source_target_pairs={{0,12},{4,8},{8,4},{12,0},{1,13},{5,9},{9,5},{13,1},{2,14},{6,10},... | collective-permute-start | bytes 196616 | tf_op jit(solution)/shard_map/ppermute | solution.py:252
  16.8 0.0 collective-permute-done.3.rec_ref
  16.8 0.8 %pair_terms.5 = bf16[128,256]{1,0:T(8,128)(2,1)S(1)} custom-call(bf16[4,2,1024]{2,1,0:T(2,128)(2,1)S(1)} %collective-permute-done.3.rec_ref, bf16[256,512]{1,0:T(8,128)(2,1)S(1)} %get-tuple-element.19.band_ref, bf16[2,128,1024]{2,1,0:T(8,128)(2,1)S(1)} %get-tuple-element.20.kept_ref, f32[2,128,1]{2,1,0:T(8,128)S(1)} %get-tuple-element.21.energy_ref, ...), custom_call_target="tpu_custom_call" | custom-call | flops 134217728 | bytes 1048576 | tf_op jit(solution)/shard_map/pair_terms/pallas_call | solution.py:193
  17.6 0.0 copy-start
  17.6 0.1 collective-permute-start.4
  17.7 0.8 %pair_terms.4 = f32[128,256]{1,0:T(8,128)S(1)} custom-call(bf16[4,2,1024]{2,1,0:T(2,128)(2,1)S(1)} %pad_maximum_fusion.rec_ref, bf16[256,512]{1,0:T(8,128)(2,1)S(1)} %get-tuple-element.19.band_ref, bf16[2,128,1024]{2,1,0:T(8,128)(2,1)S(1)} %get-tuple-element.20.kept_ref, f32[2,128,1]{2,1,0:T(8,128)S(1)} %get-tuple-element.21.energy_ref, ...), custom_call_target="tpu_custom_call" | custom-call | flops 134217728 | bytes 1048576 | tf_op jit(solution)/shard_map/pair_terms/pallas_call | solution.py:193
  18.4 0.0 collective-permute-done.8
  18.4 3.1 %collective-permute-done.6 = bf16[128,256]{1,0:T(8,128)(2,1)S(1)} collective-permute-done((bf16[128,256]{1,0:T(8,128)(2,1)S(1)}, bf16[128,256]{1,0:T(8,128)(2,1)S(1)}, u32[]{:S(2)}, u32[]{:S(2)}) %collective-permute-start.6) | collective-permute-done | bytes 65568 | tf_op jit(solution)/shard_map/ppermute | solution.py:252
  21.5 0.7 %collective-permute-done.4 = bf16[128,256]{1,0:T(8,128)(2,1)S(1)} collective-permute-done((bf16[128,256]{1,0:T(8,128)(2,1)S(1)}, bf16[128,256]{1,0:T(8,128)(2,1)S(1)}, u32[]{:S(2)}, u32[]{:S(2)}) %collective-permute-start.4) | collective-permute-done | bytes 65568 | tf_op jit(solution)/shard_map/ppermute | solution.py:252
  22.2 0.0 copy-done
  22.2 0.7 %convert_add_fusion = f32[128,256]{1,0:T(8,128)} fusion(bf16[128,256]{1,0:T(8,128)(2,1)S(1)} %collective-permute-done.8, bf16[128,256]{1,0:T(8,128)(2,1)S(1)} %collective-permute-done.6, bf16[128,256]{1,0:T(8,128)(2,1)S(1)} %collective-permute-done.4, f32[128,256]{1,0:T(8,128)S(1)} %copy-done, f32[128,256]{1,0:T(8,128)S(1)} %pair_terms.4), kind=kLoop, calls=%fused_computation | loop fusion | flops 229376 | bytes 589824 | tf_op jit(solution)/shard_map/add | solution.py:255
  (3 shorter events, 0.1 us)
Async XLA Ops:
  0.0 3.1 %copy-start.2 = (bf16[129]{0:T(256)(128)(2,1)S(1)}, bf16[129]{0:T(256)(128)(2,1)}, u32[]{:S(2)}) copy-start(bf16[129]{0:T(256)(128)(2,1)} %param.10) | copy-start | bytes 778
  0.0 5.4 %collective-permute-start.2 = (bf16[1,2,1024]{2,1,0:T(2,128)(2,1)}, bf16[1,2,1024]{2,1,0:T(2,128)(2,1)S(1)}, u32[]{:S(2)}, u32[]{:S(2)}) collective-permute-start(bf16[1,2,1024]{2,1,0:T(2,128)(2,1)} %bitcast.13), channel_id=1, source_target_pairs={{0,1},{1,0},{2,3},{3,2},{4,5},{5,4},{6,7},{7,6},{8,9},{9,8},{10,11... | collective-permute-start | bytes 12296 | tf_op jit(solution)/shard_map/ppermute | solution.py:218
  0.5 4.9 %collective-permute-start.1 = (bf16[1,2,1024]{2,1,0:T(2,128)(2,1)}, bf16[1,2,1024]{2,1,0:T(2,128)(2,1)S(1)}, u32[]{:S(2)}, u32[]{:S(2)}) collective-permute-start(bf16[1,2,1024]{2,1,0:T(2,128)(2,1)} %bitcast.14), channel_id=1, source_target_pairs={{0,2},{1,3},{2,0},{3,1},{4,6},{5,7},{6,4},{7,5},{8,10},{9,11},{10,... | collective-permute-start | bytes 12296 | tf_op jit(solution)/shard_map/ppermute | solution.py:218
  3.0 3.2 %collective-permute-start = (bf16[1,2,1024]{2,1,0:T(2,128)(2,1)}, bf16[1,2,1024]{2,1,0:T(2,128)(2,1)S(1)}, u32[]{:S(2)}, u32[]{:S(2)}) collective-permute-start(bf16[1,2,1024]{2,1,0:T(2,128)(2,1)} %bitcast.15), channel_id=1, source_target_pairs={{0,3},{1,2},{2,1},{3,0},{4,7},{5,6},{6,5},{7,4},{8,11},{9,10},{10,... | collective-permute-start | bytes 12296 | tf_op jit(solution)/shard_map/ppermute | solution.py:218
  5.4 0.9 %copy-start.1 = (bf16[2,1,1024]{2,0,1:T(2,128)(2,1)S(1)}, bf16[2,1,1024]{2,0,1:T(2,128)(2,1)}, u32[]{:S(2)}) copy-start(bf16[2,1,1024]{2,0,1:T(2,128)(2,1)} %param.9) | copy-start | bytes 12292
  6.3 4.7 %collective-permute-start.7 = (bf16[4,2,1024]{2,1,0:T(2,128)(2,1)S(1)}, bf16[4,2,1024]{2,1,0:T(2,128)(2,1)S(1)}, u32[]{:S(2)}, u32[]{:S(2)}) collective-permute-start(bf16[4,2,1024]{2,1,0:T(2,128)(2,1)S(1)} %pad_maximum_fusion.rec_ref), channel_id=1, source_target_pairs={{8,0},{12,4},{0,8},{4,12},{9,1},{13,5},{1,9},{5,13},{10,2},{14,6},... | collective-permute-start | bytes 49160 | tf_op jit(solution)/shard_map/ppermute | solution.py:248
  9.1 5.5 %collective-permute-start.5 = (bf16[4,2,1024]{2,1,0:T(2,128)(2,1)S(1)}, bf16[4,2,1024]{2,1,0:T(2,128)(2,1)S(1)}, u32[]{:S(2)}, u32[]{:S(2)}) collective-permute-start(bf16[4,2,1024]{2,1,0:T(2,128)(2,1)S(1)} %pad_maximum_fusion.rec_ref), channel_id=1, source_target_pairs={{12,0},{8,4},{4,8},{0,12},{13,1},{9,5},{5,9},{1,13},{14,2},{10,6},... | collective-permute-start | bytes 49160 | tf_op jit(solution)/shard_map/ppermute | solution.py:248
  10.4 6.4 %collective-permute-start.3 = (bf16[4,2,1024]{2,1,0:T(2,128)(2,1)S(1)}, bf16[4,2,1024]{2,1,0:T(2,128)(2,1)S(1)}, u32[]{:S(2)}, u32[]{:S(2)}) collective-permute-start(bf16[4,2,1024]{2,1,0:T(2,128)(2,1)S(1)} %pad_maximum_fusion.rec_ref), channel_id=1, source_target_pairs={{4,0},{0,4},{12,8},{8,12},{5,1},{1,5},{13,9},{9,13},{6,2},{2,6},{1... | collective-permute-start | bytes 49160 | tf_op jit(solution)/shard_map/ppermute | solution.py:248
  11.8 6.6 %collective-permute-start.8 = (bf16[128,256]{1,0:T(8,128)(2,1)S(1)}, bf16[128,256]{1,0:T(8,128)(2,1)S(1)}, u32[]{:S(2)}, u32[]{:S(2)}) collective-permute-start(bf16[128,256]{1,0:T(8,128)(2,1)S(1)} %pair_terms.7), channel_id=1, source_target_pairs={{0,8},{4,12},{8,0},{12,4},{1,9},{5,13},{9,1},{13,5},{2,10},{6,14},... | collective-permute-start | bytes 196616 | tf_op jit(solution)/shard_map/ppermute | solution.py:252
  15.4 6.2 %collective-permute-start.6 = (bf16[128,256]{1,0:T(8,128)(2,1)S(1)}, bf16[128,256]{1,0:T(8,128)(2,1)S(1)}, u32[]{:S(2)}, u32[]{:S(2)}) collective-permute-start(bf16[128,256]{1,0:T(8,128)(2,1)S(1)} %pair_terms.6), channel_id=1, source_target_pairs={{0,12},{4,8},{8,4},{12,0},{1,13},{5,9},{9,5},{13,1},{2,14},{6,10},... | collective-permute-start | bytes 196616 | tf_op jit(solution)/shard_map/ppermute | solution.py:252
  17.6 4.6 %copy-start = (f32[128,256]{1,0:T(8,128)S(1)}, f32[128,256]{1,0:T(8,128)}, u32[]{:S(2)}) copy-start(f32[128,256]{1,0:T(8,128)} %param.11) | copy-start | bytes 393220
  17.6 4.6 %collective-permute-start.4 = (bf16[128,256]{1,0:T(8,128)(2,1)S(1)}, bf16[128,256]{1,0:T(8,128)(2,1)S(1)}, u32[]{:S(2)}, u32[]{:S(2)}) collective-permute-start(bf16[128,256]{1,0:T(8,128)(2,1)S(1)} %pair_terms.5), channel_id=1, source_target_pairs={{0,4},{4,0},{8,12},{12,8},{1,5},{5,1},{9,13},{13,9},{2,6},{6,2},{1... | collective-permute-start | bytes 196616 | tf_op jit(solution)/shard_map/ppermute | solution.py:252

commit v4 on v3

--- a/solution.py
+++ b/solution.py
@@ -24,15 +24,19 @@
     return lax.dot_general(left, right, (((1,), (1,)), ((), ())), preferred_element_type=jnp.float32)
 
 
-def filter_rows(raw, band):
+def dot_nn(left, right):
+    return jnp.dot(left, right, preferred_element_type=jnp.float32)
+
+
+def filter_rows(raw, band, dot):
     rows, length = raw.shape
-    block, width = band.shape
+    width, block = max(band.shape), min(band.shape)
     halo = (width - block) // 2
     edge = jnp.zeros((rows, halo), raw.dtype)
     padded = jnp.concatenate([edge, raw, edge], axis=1)
     starts = range(0, length, block)
     stacked = jnp.concatenate([padded[:, start : start + width] for start in starts], axis=0)
-    out = dot_nt(stacked.astype(jnp.bfloat16), band)
+    out = dot(stacked.astype(jnp.bfloat16), band)
     pieces = [out[i * rows : (i + 1) * rows] for i in range(len(starts))]
     return jnp.concatenate(pieces[::-1], axis=1)
 
@@ -63,7 +67,7 @@
         copy.start()
     taps = taps_ref.shape[1]
     half = (taps - 1) // 2
-    block, width = band_ref.shape
+    width, block = band_ref.shape
     row_ref[...] = jnp.zeros_like(row_ref)
     row_ref[:, 0:taps] = taps_ref[...].astype(jnp.float32)
     spread = jnp.broadcast_to(row_ref[...], (LANES, width - LANES))
@@ -76,7 +80,9 @@
     upper = jnp.concatenate([empty, part], axis=1)
     lower = jnp.concatenate([part, empty], axis=1)
     band = jnp.concatenate([upper, lower], axis=0).astype(jnp.bfloat16)
-    band_ref[...] = band
+    upper = jnp.concatenate([empty, part.T], axis=0)
+    lower = jnp.concatenate([part.T, empty], axis=0)
+    band_ref[...] = jnp.concatenate([upper, lower], axis=1).astype(jnp.bfloat16)
     here = lax.axis_index("row")
     owner_copy.wait()
     order_copy.wait()
@@ -88,7 +94,7 @@
         chosen = jnp.where(place == order, 1.0, 0.0).T.astype(jnp.bfloat16)
         copies[window].wait()
         raw = jnp.dot(chosen, raw_ref[window], preferred_element_type=jnp.float32)
-        kept = filter_rows(raw.astype(jnp.bfloat16), band).astype(jnp.bfloat16)
+        kept = filter_rows(raw.astype(jnp.bfloat16), band, dot_nt).astype(jnp.bfloat16)
         kept_ref[window] = kept
         squares = jnp.square(kept.astype(jnp.float32))
         energy_ref[window] = jnp.sum(squares, axis=1, keepdims=True)
@@ -104,7 +110,7 @@
         out_shape=(
             jax.ShapeDtypeStruct((windows, count, length), jnp.bfloat16),
             jax.ShapeDtypeStruct((windows, count, 1), jnp.float32),
-            jax.ShapeDtypeStruct((block, width), jnp.bfloat16),
+            jax.ShapeDtypeStruct((width, block), jnp.bfloat16),
             jax.ShapeDtypeStruct((1, LANES), jnp.int32),
         ),
         in_specs=[HBM, HBM, HBM, VMEM],
@@ -127,26 +133,25 @@
 
 
 def window_terms(windows, rec_ref, band_ref, kept_ref, energy_ref, hankel_ref):
-    receivers, _, length = rec_ref.shape
-    count = len(windows)
-    rows = receivers * count
-    raw = [rec_ref[q, windows[0] : windows[0] + count].astype(jnp.float32) for q in range(receivers)]
-    rec = filter_rows(jnp.concatenate(raw, axis=0), band_ref[...])
+    receivers, every, length = rec_ref.shape
+    rows = receivers * every
+    raw = jnp.concatenate([rec_ref[q].astype(jnp.float32) for q in range(receivers)], axis=0)
+    rec = filter_rows(raw, band_ref[...], dot_nn)
     rec = rec.astype(jnp.bfloat16).astype(jnp.float32)
     rec_energy = jnp.sum(jnp.square(rec), axis=1, keepdims=True)
     padded = jnp.concatenate([rec, jnp.zeros((rows, LANES), jnp.float32)], axis=1)
     width = length + LANES
-    for i in range(count):
+    for window in windows:
         for q in range(receivers):
-            at = q * count + i
+            at = q * every + window
             spread = jnp.broadcast_to(padded[at : at + 1], (LAGS, width))
             shifted = pltpu.roll(spread, width - LAGS // 2, 1, stride=1, stride_axis=0)
-            hankel_ref[windows[i], q * LAGS : (q + 1) * LAGS] = shifted[:, :length].astype(jnp.bfloat16)
+            hankel_ref[window, q * LAGS : (q + 1) * LAGS] = shifted[:, :length].astype(jnp.bfloat16)
     lane = lax.broadcasted_iota(jnp.int32, (rows, receivers * LAGS), 1) // LAGS
     row = lax.broadcasted_iota(jnp.int32, (rows, receivers * LAGS), 0)
     total = None
-    for i, window in enumerate(windows):
-        own = jnp.where(row == lane * count + i, rec_energy, 0.0)
+    for window in windows:
+        own = jnp.where(row == lane * every + window, rec_energy, 0.0)
         across = jnp.sum(own, axis=0, keepdims=True)
         lagged = dot_nt(kept_ref[window], hankel_ref[window])
         ratio = lagged * lax.rsqrt(energy_ref[window] * across + 1e-06)
@@ -168,22 +173,32 @@
     mine = mine_ref[0:1, 0:1][0, 0]
     every = (1 << windows) - 1
 
+    @pl.when(mine == 0)
+    def _():
+        out_ref[...] = jnp.zeros_like(out_ref)
+
     @pl.when(mine == every)
     def _():
         out_ref[...] = terms(range(windows)).astype(out_ref.dtype)
 
-    @pl.when(mine != every)
+    if windows == 2:
+        for window in range(windows):
+
+            @pl.when(mine == 1 << window)
+            def _():
+                out_ref[...] = terms([window]).astype(out_ref.dtype)
+
+        return
+
+    @pl.when((mine != 0) & (mine != every))
     def _():
         total_ref[...] = jnp.zeros_like(total_ref)
-
-    for window in range(windows):
-
-        @pl.when((mine != every) & ((mine >> window) & 1 == 1))
-        def _():
-            total_ref[...] += terms(range(window, window + 1))
-
-    @pl.when(mine != every)
-    def _():
+        for window in range(windows):
+
+            @pl.when((mine >> window) & 1 == 1)
+            def _():
+                total_ref[...] += terms([window])
+
         out_ref[...] = total_ref[...].astype(out_ref.dtype)
 
 

time: 22.9 us -> 22.8 us (level)
  waiting for transfers between devices: 5.77 us -> 6.39 us
  Pallas kernels: 5.36 us -> 4.96 us
    ppermute x3, waiting for transfers between devices: 3.76 us -> 4.17 us  [shards(): lax.ppermute(terms(arrived[step], dtype=jnp.bfloat16), 'row', pairs)]
    pallas_call x4, Pallas kernels: 3.06 us -> 2.66 us  [pair_terms(): pl.pallas_call(pair_kernel, out_shape=jax.ShapeDtypeStruct((count, receiv...]
  transfers between devices with their start and end apart: 9 -> 9, of which waited for: 5 -> 5; matrix products, arithmetic and copies ran while one was open for 0% -> 0% of each run, Pallas kernels for 23% -> 22%
where the time goes in v4:
time: 22.8 us; the launch traced here: 23 us
  starting transfers between devices  10.8 us (47%)
  waiting for transfers between devices  6.39 us (28%)
  Pallas kernels  4.96 us (22%)
  other arithmetic  0.74 us (3%)
    ppermute x3, starting transfers between devices, shards(): arrived[step] = lax.ppermute(receivers, 'row', pairs)  4.3 us
    ppermute x3, waiting for transfers between devices, shards(): lax.ppermute(terms(arrived[step], dtype=jnp.bfloat16), 'row', pairs)  4.17 us
    ppermute x3, starting transfers between devices, shards(): lax.ppermute(terms(arrived[step], dtype=jnp.bfloat16), 'row', pairs)  3.39 us
    ppermute x3, starting transfers between devices, gather_columns(): lax.ppermute(piece, 'col', [(i, i ^ step) for i in range(columns)])  3.08 us
    pallas_call x4, Pallas kernels, pair_terms(): pl.pallas_call(pair_kernel, out_shape=jax.ShapeDtypeStruct((count, receiv...  2.66 us
    pallas_call x1, Pallas kernels, prepare_sources(): pl.pallas_call(source_kernel, out_shape=(jax.ShapeDtypeStruct((windows, c...  2.29 us
    ppermute x3, waiting for transfers between devices, shards(): arrived[step] = lax.ppermute(receivers, 'row', pairs)  1.38 us
    ppermute x3, waiting for transfers between devices, gather_columns(): lax.ppermute(piece, 'col', [(i, i ^ step) for i in range(columns)])  0.84 us
  transfers between devices with their start and end apart: 9, of which 5 were waited for; matrix products, arithmetic and copies ran while one was open for 0% of the time, Pallas kernels for 22%

profile of v4, /device:TPU:0, one launch (start us, length us, event | category | flops | bytes accessed | tf_op | source)
XLA Modules:
  0.0 23.0 jit_solution(12445382113955165818)
XLA Ops:
  0.0 0.0 copy-start.2
  0.0 0.5 %collective-permute-start.2 = (bf16[1,2,1024]{2,1,0:T(2,128)(2,1)}, bf16[1,2,1024]{2,1,0:T(2,128)(2,1)S(1)}, u32[]{:S(2)}, u32[]{:S(2)}) collective-permute-start(bf16[1,2,1024]{2,1,0:T(2,128)(2,1)} %bitcast.13), channel_id=1, source_target_pairs={{0,1},{1,0},{2,3},{3,2},{4,5},{5,4},{6,7},{7,6},{8,9},{9,8},{10,11... | collective-permute-start | bytes 12296 | tf_op jit(solution)/shard_map/ppermute | solution.py:233
  0.5 2.5 %collective-permute-start.1 = (bf16[1,2,1024]{2,1,0:T(2,128)(2,1)}, bf16[1,2,1024]{2,1,0:T(2,128)(2,1)S(1)}, u32[]{:S(2)}, u32[]{:S(2)}) collective-permute-start(bf16[1,2,1024]{2,1,0:T(2,128)(2,1)} %bitcast.14), channel_id=1, source_target_pairs={{0,2},{1,3},{2,0},{3,1},{4,6},{5,7},{6,4},{7,5},{8,10},{9,11},{10,... | collective-permute-start | bytes 12296 | tf_op jit(solution)/shard_map/ppermute | solution.py:233
  3.0 0.1 collective-permute-start
  3.1 0.0 copy-done.2
  3.1 2.3 %prepare_sources.1 = (bf16[2,128,1024]{2,1,0:T(8,128)(2,1)S(1)}, f32[2,128,1]{2,1,0:T(8,128)S(1)}, bf16[512,256]{1,0:T(8,128)(2,1)S(1)}, s32[1,128]{1,0:T(1,128)S(1)}) custom-call(s32[1,2]{1,0:T(1,128)} %bitcast.17, s32[2,1,128]{2,1,0:T(1,128)} %order_hbm.1, bf16[2,128,1024]{2,1,0:T(8,128)(2,1)} %bitcast.16, bf16[1,129]{1,0:T(2,128)(2,1)S(1)} %reshape.3.taps_ref), custom_call_target="tpu_custom_call" | custom-call | flops 335544320 | bytes 1048576 | tf_op jit(solution)/shard_map/prepare_sources/pallas_call | solution.py:108
  5.4 0.0 copy-start.1
  5.4 0.0 collective-permute-done.2
  5.4 0.0 collective-permute-done.1
  5.4 0.8 %collective-permute-done = bf16[1,2,1024]{2,1,0:T(2,128)(2,1)S(1)} collective-permute-done((bf16[1,2,1024]{2,1,0:T(2,128)(2,1)}, bf16[1,2,1024]{2,1,0:T(2,128)(2,1)S(1)}, u32[]{:S(2)}, u32[]{:S(2)}) %collective-permute-start) | collective-permute-done | bytes 4128 | tf_op jit(solution)/shard_map/ppermute | solution.py:233
  6.3 0.0 copy-done.1
  6.3 2.7 %collective-permute-start.7 = (bf16[4,2,1024]{2,1,0:T(2,128)(2,1)S(1)}, bf16[4,2,1024]{2,1,0:T(2,128)(2,1)S(1)}, u32[]{:S(2)}, u32[]{:S(2)}) collective-permute-start(bf16[4,2,1024]{2,1,0:T(2,128)(2,1)S(1)} %pad_maximum_fusion.rec_ref), channel_id=1, source_target_pairs={{8,0},{12,4},{0,8},{4,12},{9,1},{13,5},{1,9},{5,13},{10,2},{14,6},... | collective-permute-start | bytes 49160 | tf_op jit(solution)/shard_map/ppermute | solution.py:263
  9.1 1.3 %collective-permute-start.5 = (bf16[4,2,1024]{2,1,0:T(2,128)(2,1)S(1)}, bf16[4,2,1024]{2,1,0:T(2,128)(2,1)S(1)}, u32[]{:S(2)}, u32[]{:S(2)}) collective-permute-start(bf16[4,2,1024]{2,1,0:T(2,128)(2,1)S(1)} %pad_maximum_fusion.rec_ref), channel_id=1, source_target_pairs={{12,0},{8,4},{4,8},{0,12},{13,1},{9,5},{5,9},{1,13},{14,2},{10,6},... | collective-permute-start | bytes 49160 | tf_op jit(solution)/shard_map/ppermute | solution.py:263
  10.4 0.2 %collective-permute-start.3 = (bf16[4,2,1024]{2,1,0:T(2,128)(2,1)S(1)}, bf16[4,2,1024]{2,1,0:T(2,128)(2,1)S(1)}, u32[]{:S(2)}, u32[]{:S(2)}) collective-permute-start(bf16[4,2,1024]{2,1,0:T(2,128)(2,1)S(1)} %pad_maximum_fusion.rec_ref), channel_id=1, source_target_pairs={{4,0},{0,4},{12,8},{8,12},{5,1},{1,5},{13,9},{9,13},{6,2},{2,6},{1... | collective-permute-start | bytes 49160 | tf_op jit(solution)/shard_map/ppermute | solution.py:263
  10.6 0.4 %collective-permute-done.7.rec_ref = bf16[4,2,1024]{2,1,0:T(2,128)(2,1)S(1)} collective-permute-done((bf16[4,2,1024]{2,1,0:T(2,128)(2,1)S(1)}, bf16[4,2,1024]{2,1,0:T(2,128)(2,1)S(1)}, u32[]{:S(2)}, u32[]{:S(2)}) %collective-permute-start.7) | collective-permute-done | bytes 16416 | tf_op jit(solution)/shard_map/ppermute | solution.py:263
  11.0 0.7 %pair_terms.7 = bf16[128,256]{1,0:T(8,128)(2,1)S(1)} custom-call(bf16[4,2,1024]{2,1,0:T(2,128)(2,1)S(1)} %collective-permute-done.7.rec_ref, bf16[512,256]{1,0:T(8,128)(2,1)S(1)} %get-tuple-element.19.band_ref, bf16[2,128,1024]{2,1,0:T(8,128)(2,1)S(1)} %get-tuple-element.20.kept_ref, f32[2,128,1]{2,1,0:T(8,128)S(1)} %get-tuple-element.21.energy_ref, ...), custom_call_target="tpu_custom_call" | custom-call | flops 134217728 | bytes 1048576 | tf_op jit(solution)/shard_map/pair_terms/pallas_call | solution.py:208
  11.7 2.1 %collective-permute-start.8 = (bf16[128,256]{1,0:T(8,128)(2,1)S(1)}, bf16[128,256]{1,0:T(8,128)(2,1)S(1)}, u32[]{:S(2)}, u32[]{:S(2)}) collective-permute-start(bf16[128,256]{1,0:T(8,128)(2,1)S(1)} %pair_terms.7), channel_id=1, source_target_pairs={{0,8},{4,12},{8,0},{12,4},{1,9},{5,13},{9,1},{13,5},{2,10},{6,14},... | collective-permute-start | bytes 196616 | tf_op jit(solution)/shard_map/ppermute | solution.py:267
  13.8 1.0 %collective-permute-done.5.rec_ref = bf16[4,2,1024]{2,1,0:T(2,128)(2,1)S(1)} collective-permute-done((bf16[4,2,1024]{2,1,0:T(2,128)(2,1)S(1)}, bf16[4,2,1024]{2,1,0:T(2,128)(2,1)S(1)}, u32[]{:S(2)}, u32[]{:S(2)}) %collective-permute-start.5) | collective-permute-done | bytes 16416 | tf_op jit(solution)/shard_map/ppermute | solution.py:263
  14.8 0.7 %pair_terms.6 = bf16[128,256]{1,0:T(8,128)(2,1)S(1)} custom-call(bf16[4,2,1024]{2,1,0:T(2,128)(2,1)S(1)} %collective-permute-done.5.rec_ref, bf16[512,256]{1,0:T(8,128)(2,1)S(1)} %get-tuple-element.19.band_ref, bf16[2,128,1024]{2,1,0:T(8,128)(2,1)S(1)} %get-tuple-element.20.kept_ref, f32[2,128,1]{2,1,0:T(8,128)S(1)} %get-tuple-element.21.energy_ref, ...), custom_call_target="tpu_custom_call" | custom-call | flops 134217728 | bytes 1048576 | tf_op jit(solution)/shard_map/pair_terms/pallas_call | solution.py:208
  15.5 1.2 %collective-permute-start.6 = (bf16[128,256]{1,0:T(8,128)(2,1)S(1)}, bf16[128,256]{1,0:T(8,128)(2,1)S(1)}, u32[]{:S(2)}, u32[]{:S(2)}) collective-permute-start(bf16[128,256]{1,0:T(8,128)(2,1)S(1)} %pair_terms.6), channel_id=1, source_target_pairs={{0,12},{4,8},{8,4},{12,0},{1,13},{5,9},{9,5},{13,1},{2,14},{6,10},... | collective-permute-start | bytes 196616 | tf_op jit(solution)/shard_map/ppermute | solution.py:267
  16.7 0.0 collective-permute-done.3.rec_ref
  16.7 0.7 %pair_terms.5 = bf16[128,256]{1,0:T(8,128)(2,1)S(1)} custom-call(bf16[4,2,1024]{2,1,0:T(2,128)(2,1)S(1)} %collective-permute-done.3.rec_ref, bf16[512,256]{1,0:T(8,128)(2,1)S(1)} %get-tuple-element.19.band_ref, bf16[2,128,1024]{2,1,0:T(8,128)(2,1)S(1)} %get-tuple-element.20.kept_ref, f32[2,128,1]{2,1,0:T(8,128)S(1)} %get-tuple-element.21.energy_ref, ...), custom_call_target="tpu_custom_call" | custom-call | flops 134217728 | bytes 1048576 | tf_op jit(solution)/shard_map/pair_terms/pallas_call | solution.py:208
  17.4 0.0 copy-start
  17.4 0.1 collective-permute-start.4
  17.5 0.7 %pair_terms.4 = f32[128,256]{1,0:T(8,128)S(1)} custom-call(bf16[4,2,1024]{2,1,0:T(2,128)(2,1)S(1)} %pad_maximum_fusion.rec_ref, bf16[512,256]{1,0:T(8,128)(2,1)S(1)} %get-tuple-element.19.band_ref, bf16[2,128,1024]{2,1,0:T(8,128)(2,1)S(1)} %get-tuple-element.20.kept_ref, f32[2,128,1]{2,1,0:T(8,128)S(1)} %get-tuple-element.21.energy_ref, ...), custom_call_target="tpu_custom_call" | custom-call | flops 134217728 | bytes 1048576 | tf_op jit(solution)/shard_map/pair_terms/pallas_call | solution.py:208
  18.1 0.0 collective-permute-done.8
  18.1 3.5 %collective-permute-done.6 = bf16[128,256]{1,0:T(8,128)(2,1)S(1)} collective-permute-done((bf16[128,256]{1,0:T(8,128)(2,1)S(1)}, bf16[128,256]{1,0:T(8,128)(2,1)S(1)}, u32[]{:S(2)}, u32[]{:S(2)}) %collective-permute-start.6) | collective-permute-done | bytes 65568 | tf_op jit(solution)/shard_map/ppermute | solution.py:267
  21.7 0.6 %collective-permute-done.4 = bf16[128,256]{1,0:T(8,128)(2,1)S(1)} collective-permute-done((bf16[128,256]{1,0:T(8,128)(2,1)S(1)}, bf16[128,256]{1,0:T(8,128)(2,1)S(1)}, u32[]{:S(2)}, u32[]{:S(2)}) %collective-permute-start.4) | collective-permute-done | bytes 65568 | tf_op jit(solution)/shard_map/ppermute | solution.py:267
  22.3 0.0 copy-done
  22.3 0.7 %convert_add_fusion = f32[128,256]{1,0:T(8,128)} fusion(bf16[128,256]{1,0:T(8,128)(2,1)S(1)} %collective-permute-done.8, bf16[128,256]{1,0:T(8,128)(2,1)S(1)} %collective-permute-done.6, bf16[128,256]{1,0:T(8,128)(2,1)S(1)} %collective-permute-done.4, f32[128,256]{1,0:T(8,128)S(1)} %copy-done, f32[128,256]{1,0:T(8,128)S(1)} %pair_terms.4), kind=kLoop, calls=%fused_computation | loop fusion | flops 229376 | bytes 589824 | tf_op jit(solution)/shard_map/add | solution.py:270
  (3 shorter events, 0.1 us)
Async XLA Ops:
  0.0 3.1 %copy-start.2 = (bf16[129]{0:T(256)(128)(2,1)S(1)}, bf16[129]{0:T(256)(128)(2,1)}, u32[]{:S(2)}) copy-start(bf16[129]{0:T(256)(128)(2,1)} %param.10) | copy-start | bytes 778
  0.0 5.4 %collective-permute-start.2 = (bf16[1,2,1024]{2,1,0:T(2,128)(2,1)}, bf16[1,2,1024]{2,1,0:T(2,128)(2,1)S(1)}, u32[]{:S(2)}, u32[]{:S(2)}) collective-permute-start(bf16[1,2,1024]{2,1,0:T(2,128)(2,1)} %bitcast.13), channel_id=1, source_target_pairs={{0,1},{1,0},{2,3},{3,2},{4,5},{5,4},{6,7},{7,6},{8,9},{9,8},{10,11... | collective-permute-start | bytes 12296 | tf_op jit(solution)/shard_map/ppermute | solution.py:233
  0.5 4.9 %collective-permute-start.1 = (bf16[1,2,1024]{2,1,0:T(2,128)(2,1)}, bf16[1,2,1024]{2,1,0:T(2,128)(2,1)S(1)}, u32[]{:S(2)}, u32[]{:S(2)}) collective-permute-start(bf16[1,2,1024]{2,1,0:T(2,128)(2,1)} %bitcast.14), channel_id=1, source_target_pairs={{0,2},{1,3},{2,0},{3,1},{4,6},{5,7},{6,4},{7,5},{8,10},{9,11},{10,... | collective-permute-start | bytes 12296 | tf_op jit(solution)/shard_map/ppermute | solution.py:233
  3.0 3.2 %collective-permute-start = (bf16[1,2,1024]{2,1,0:T(2,128)(2,1)}, bf16[1,2,1024]{2,1,0:T(2,128)(2,1)S(1)}, u32[]{:S(2)}, u32[]{:S(2)}) collective-permute-start(bf16[1,2,1024]{2,1,0:T(2,128)(2,1)} %bitcast.15), channel_id=1, source_target_pairs={{0,3},{1,2},{2,1},{3,0},{4,7},{5,6},{6,5},{7,4},{8,11},{9,10},{10,... | collective-permute-start | bytes 12296 | tf_op jit(solution)/shard_map/ppermute | solution.py:233
  5.4 0.9 %copy-start.1 = (bf16[2,1,1024]{2,0,1:T(2,128)(2,1)S(1)}, bf16[2,1,1024]{2,0,1:T(2,128)(2,1)}, u32[]{:S(2)}) copy-start(bf16[2,1,1024]{2,0,1:T(2,128)(2,1)} %param.9) | copy-start | bytes 12292
  6.3 4.7 %collective-permute-start.7 = (bf16[4,2,1024]{2,1,0:T(2,128)(2,1)S(1)}, bf16[4,2,1024]{2,1,0:T(2,128)(2,1)S(1)}, u32[]{:S(2)}, u32[]{:S(2)}) collective-permute-start(bf16[4,2,1024]{2,1,0:T(2,128)(2,1)S(1)} %pad_maximum_fusion.rec_ref), channel_id=1, source_target_pairs={{8,0},{12,4},{0,8},{4,12},{9,1},{13,5},{1,9},{5,13},{10,2},{14,6},... | collective-permute-start | bytes 49160 | tf_op jit(solution)/shard_map/ppermute | solution.py:263
  9.1 5.7 %collective-permute-start.5 = (bf16[4,2,1024]{2,1,0:T(2,128)(2,1)S(1)}, bf16[4,2,1024]{2,1,0:T(2,128)(2,1)S(1)}, u32[]{:S(2)}, u32[]{:S(2)}) collective-permute-start(bf16[4,2,1024]{2,1,0:T(2,128)(2,1)S(1)} %pad_maximum_fusion.rec_ref), channel_id=1, source_target_pairs={{12,0},{8,4},{4,8},{0,12},{13,1},{9,5},{5,9},{1,13},{14,2},{10,6},... | collective-permute-start | bytes 49160 | tf_op jit(solution)/shard_map/ppermute | solution.py:263
  10.4 6.3 %collective-permute-start.3 = (bf16[4,2,1024]{2,1,0:T(2,128)(2,1)S(1)}, bf16[4,2,1024]{2,1,0:T(2,128)(2,1)S(1)}, u32[]{:S(2)}, u32[]{:S(2)}) collective-permute-start(bf16[4,2,1024]{2,1,0:T(2,128)(2,1)S(1)} %pad_maximum_fusion.rec_ref), channel_id=1, source_target_pairs={{4,0},{0,4},{12,8},{8,12},{5,1},{1,5},{13,9},{9,13},{6,2},{2,6},{1... | collective-permute-start | bytes 49160 | tf_op jit(solution)/shard_map/ppermute | solution.py:263
  11.7 6.4 %collective-permute-start.8 = (bf16[128,256]{1,0:T(8,128)(2,1)S(1)}, bf16[128,256]{1,0:T(8,128)(2,1)S(1)}, u32[]{:S(2)}, u32[]{:S(2)}) collective-permute-start(bf16[128,256]{1,0:T(8,128)(2,1)S(1)} %pair_terms.7), channel_id=1, source_target_pairs={{0,8},{4,12},{8,0},{12,4},{1,9},{5,13},{9,1},{13,5},{2,10},{6,14},... | collective-permute-start | bytes 196616 | tf_op jit(solution)/shard_map/ppermute | solution.py:267
  15.5 6.2 %collective-permute-start.6 = (bf16[128,256]{1,0:T(8,128)(2,1)S(1)}, bf16[128,256]{1,0:T(8,128)(2,1)S(1)}, u32[]{:S(2)}, u32[]{:S(2)}) collective-permute-start(bf16[128,256]{1,0:T(8,128)(2,1)S(1)} %pair_terms.6), channel_id=1, source_target_pairs={{0,12},{4,8},{8,4},{12,0},{1,13},{5,9},{9,5},{13,1},{2,14},{6,10},... | collective-permute-start | bytes 196616 | tf_op jit(solution)/shard_map/ppermute | solution.py:267
  17.4 4.9 %copy-start = (f32[128,256]{1,0:T(8,128)S(1)}, f32[128,256]{1,0:T(8,128)}, u32[]{:S(2)}) copy-start(f32[128,256]{1,0:T(8,128)} %param.11) | copy-start | bytes 393220
  17.4 4.9 %collective-permute-start.4 = (bf16[128,256]{1,0:T(8,128)(2,1)S(1)}, bf16[128,256]{1,0:T(8,128)(2,1)S(1)}, u32[]{:S(2)}, u32[]{:S(2)}) collective-permute-start(bf16[128,256]{1,0:T(8,128)(2,1)S(1)} %pair_terms.5), channel_id=1, source_target_pairs={{0,4},{4,0},{8,12},{12,8},{1,5},{5,1},{9,13},{13,9},{2,6},{6,2},{1... | collective-permute-start | bytes 196616 | tf_op jit(solution)/shard_map/ppermute | solution.py:267

commit v5 on v4

--- a/solution.py
+++ b/solution.py
@@ -240,6 +240,10 @@
     return jnp.concatenate(pieces, axis=0)
 
 
+def far_first(rows):
+    return [*range(2, rows), 1]
+
+
 def shards(mesh_shape, src_raw, block_owner, chan_order, rec_raw, fir_taps, stacks):
     rows, columns = mesh_shape["row"], mesh_shape["col"]
     prepared = prepare_sources(block_owner, chan_order, src_raw[0], fir_taps)
@@ -256,15 +260,15 @@
     def partner(i, step):
         return i ^ step if rows & (rows - 1) == 0 else (i + step) % rows
 
-    order = [1, *range(rows - 1, 1, -1)]
-    arrived = {}
-    for step in order:
-        pairs = [(partner(i, step), i) for i in range(rows)]
-        arrived[step] = lax.ppermute(receivers, "row", pairs)
-    parts = []
-    for step in order:
-        pairs = [(i, partner(i, step)) for i in range(rows)]
-        parts.append(lax.ppermute(terms(arrived[step], dtype=jnp.bfloat16), "row", pairs))
+    def send(value, step):
+        return lax.ppermute(value, "row", [(i, partner(i, step)) for i in range(rows)])
+
+    def fetch(value, step):
+        return lax.ppermute(value, "row", [(partner(i, step), i) for i in range(rows)])
+
+    order = far_first(rows)
+    arrived = {step: fetch(receivers, step) for step in order}
+    parts = [send(terms(arrived[step], dtype=jnp.bfloat16), step) for step in order]
     total = stacks + terms(receivers, dtype=jnp.float32)
     for part in parts:
         total = total + part.astype(jnp.float32)
@@ -281,5 +285,8 @@
         P(("grp", "col"), "row"),
     )
     out_specs = P(("grp", "col"), "row")
-    body = functools.partial(shards, dict(mesh.shape))
+
+    def body(*args):
+        return shards(dict(mesh.shape), *args)
+
     return jax.shard_map(body, mesh=mesh, in_specs=in_specs, out_specs=out_specs, check_vma=False)

time: 22.8 us -> 23 us (level); the launches traced: 23 us -> 22.8 us
  waiting for transfers between devices: 6.39 us -> 5.83 us
  starting transfers between devices: 10.8 us -> 11.1 us
    ppermute x6, waiting for transfers between devices: 5.55 us -> 4.98 us  [the longest x3 4.47 us: send(): lax.ppermute(value, 'row', [(i, partner(i, step)) for i in range(rows)])]
    ppermute x6, starting transfers between devices: 7.69 us -> 8.06 us  [the longest x3 4.3 us: fetch(): lax.ppermute(value, 'row', [(partner(i, step), i) for i in range(rows)])]
  transfers between devices with their start and end apart: 9 -> 9, of which waited for: 5 -> 4; matrix products, arithmetic and copies ran while one was open for 0% -> 0% of each run, Pallas kernels for 22% -> 22%
where the time goes in v5:
time: 23 us; the launch traced here: 22.8 us
  starting transfers between devices  11.1 us (48%)
  waiting for transfers between devices  5.83 us (25%)
  Pallas kernels  4.96 us (22%)
  other arithmetic  0.74 us (3%)
    ppermute x3, waiting for transfers between devices, send(): lax.ppermute(value, 'row', [(i, partner(i, step)) for i in range(rows)])  4.47 us
    ppermute x3, starting transfers between devices, fetch(): lax.ppermute(value, 'row', [(partner(i, step), i) for i in range(rows)])  4.3 us
    ppermute x3, starting transfers between devices, send(): lax.ppermute(value, 'row', [(i, partner(i, step)) for i in range(rows)])  3.76 us
    ppermute x3, starting transfers between devices, gather_columns(): lax.ppermute(piece, 'col', [(i, i ^ step) for i in range(columns)])  3.08 us
    pallas_call x4, Pallas kernels, pair_terms(): pl.pallas_call(pair_kernel, out_shape=jax.ShapeDtypeStruct((count, receiv...  2.66 us
    pallas_call x1, Pallas kernels, prepare_sources(): pl.pallas_call(source_kernel, out_shape=(jax.ShapeDtypeStruct((windows, c...  2.29 us
    ppermute x3, waiting for transfers between devices, gather_columns(): lax.ppermute(piece, 'col', [(i, i ^ step) for i in range(columns)])  0.84 us
    add x1, other arithmetic, shards(): total = total + part.astype(jnp.float32)  0.69 us
  transfers between devices with their start and end apart: 9, of which 4 were waited for; matrix products, arithmetic and copies ran while one was open for 0% of the time, Pallas kernels for 22%

profile of v5, /device:TPU:0, one launch (start us, length us, event | category | flops | bytes accessed | tf_op | source)
XLA Modules:
  0.0 22.8 jit_solution(4411454371182551255)
XLA Ops:
  0.0 0.0 copy-start.2
  0.0 0.5 %collective-permute-start.2 = (bf16[1,2,1024]{2,1,0:T(2,128)(2,1)}, bf16[1,2,1024]{2,1,0:T(2,128)(2,1)S(1)}, u32[]{:S(2)}, u32[]{:S(2)}) collective-permute-start(bf16[1,2,1024]{2,1,0:T(2,128)(2,1)} %bitcast.13), channel_id=1, source_target_pairs={{0,1},{1,0},{2,3},{3,2},{4,5},{5,4},{6,7},{7,6},{8,9},{9,8},{10,11... | collective-permute-start | bytes 12296 | tf_op jit(solution)/shard_map/ppermute | solution.py:233
  0.5 2.5 %collective-permute-start.1 = (bf16[1,2,1024]{2,1,0:T(2,128)(2,1)}, bf16[1,2,1024]{2,1,0:T(2,128)(2,1)S(1)}, u32[]{:S(2)}, u32[]{:S(2)}) collective-permute-start(bf16[1,2,1024]{2,1,0:T(2,128)(2,1)} %bitcast.14), channel_id=1, source_target_pairs={{0,2},{1,3},{2,0},{3,1},{4,6},{5,7},{6,4},{7,5},{8,10},{9,11},{10,... | collective-permute-start | bytes 12296 | tf_op jit(solution)/shard_map/ppermute | solution.py:233
  3.0 0.1 collective-permute-start
  3.1 0.0 copy-done.2
  3.1 2.3 %prepare_sources.1 = (bf16[2,128,1024]{2,1,0:T(8,128)(2,1)S(1)}, f32[2,128,1]{2,1,0:T(8,128)S(1)}, bf16[512,256]{1,0:T(8,128)(2,1)S(1)}, s32[1,128]{1,0:T(1,128)S(1)}) custom-call(s32[1,2]{1,0:T(1,128)} %bitcast.17, s32[2,1,128]{2,1,0:T(1,128)} %order_hbm.1, bf16[2,128,1024]{2,1,0:T(8,128)(2,1)} %bitcast.16, bf16[1,129]{1,0:T(2,128)(2,1)S(1)} %reshape.3.taps_ref), custom_call_target="tpu_custom_call" | custom-call | flops 335544320 | bytes 1048576 | tf_op jit(solution)/shard_map/prepare_sources/pallas_call | solution.py:108
  5.4 0.0 copy-start.1
  5.4 0.0 collective-permute-done.2
  5.4 0.0 collective-permute-done.1
  5.4 0.8 %collective-permute-done = bf16[1,2,1024]{2,1,0:T(2,128)(2,1)S(1)} collective-permute-done((bf16[1,2,1024]{2,1,0:T(2,128)(2,1)}, bf16[1,2,1024]{2,1,0:T(2,128)(2,1)S(1)}, u32[]{:S(2)}, u32[]{:S(2)}) %collective-permute-start) | collective-permute-done | bytes 4128 | tf_op jit(solution)/shard_map/ppermute | solution.py:233
  6.3 0.0 copy-done.1
  6.3 1.7 %collective-permute-start.7 = (bf16[4,2,1024]{2,1,0:T(2,128)(2,1)S(1)}, bf16[4,2,1024]{2,1,0:T(2,128)(2,1)S(1)}, u32[]{:S(2)}, u32[]{:S(2)}) collective-permute-start(bf16[4,2,1024]{2,1,0:T(2,128)(2,1)S(1)} %pad_maximum_fusion.rec_ref), channel_id=1, source_target_pairs={{4,0},{0,4},{12,8},{8,12},{5,1},{1,5},{13,9},{9,13},{6,2},{2,6},{1... | collective-permute-start | bytes 49160 | tf_op jit(solution)/shard_map/ppermute | solution.py:267
  8.1 2.5 %collective-permute-start.5 = (bf16[4,2,1024]{2,1,0:T(2,128)(2,1)S(1)}, bf16[4,2,1024]{2,1,0:T(2,128)(2,1)S(1)}, u32[]{:S(2)}, u32[]{:S(2)}) collective-permute-start(bf16[4,2,1024]{2,1,0:T(2,128)(2,1)S(1)} %pad_maximum_fusion.rec_ref), channel_id=1, source_target_pairs={{12,0},{8,4},{4,8},{0,12},{13,1},{9,5},{5,9},{1,13},{14,2},{10,6},... | collective-permute-start | bytes 49160 | tf_op jit(solution)/shard_map/ppermute | solution.py:267
  10.5 0.1 collective-permute-start.3
  10.6 0.0 collective-permute-done.7.rec_ref
  10.6 0.7 %pair_terms.7 = bf16[128,256]{1,0:T(8,128)(2,1)S(1)} custom-call(bf16[4,2,1024]{2,1,0:T(2,128)(2,1)S(1)} %collective-permute-done.7.rec_ref, bf16[512,256]{1,0:T(8,128)(2,1)S(1)} %get-tuple-element.19.band_ref, bf16[2,128,1024]{2,1,0:T(8,128)(2,1)S(1)} %get-tuple-element.20.kept_ref, f32[2,128,1]{2,1,0:T(8,128)S(1)} %get-tuple-element.21.energy_ref, ...), custom_call_target="tpu_custom_call" | custom-call | flops 134217728 | bytes 1048576 | tf_op jit(solution)/shard_map/pair_terms/pallas_call | solution.py:208
  11.3 1.9 %collective-permute-start.8 = (bf16[128,256]{1,0:T(8,128)(2,1)S(1)}, bf16[128,256]{1,0:T(8,128)(2,1)S(1)}, u32[]{:S(2)}, u32[]{:S(2)}) collective-permute-start(bf16[128,256]{1,0:T(8,128)(2,1)S(1)} %pair_terms.7), channel_id=1, source_target_pairs={{0,4},{4,0},{8,12},{12,8},{1,5},{5,1},{9,13},{13,9},{2,6},{6,2},{1... | collective-permute-start | bytes 196616 | tf_op jit(solution)/shard_map/ppermute | solution.py:264
  13.2 0.5 %collective-permute-done.5.rec_ref = bf16[4,2,1024]{2,1,0:T(2,128)(2,1)S(1)} collective-permute-done((bf16[4,2,1024]{2,1,0:T(2,128)(2,1)S(1)}, bf16[4,2,1024]{2,1,0:T(2,128)(2,1)S(1)}, u32[]{:S(2)}, u32[]{:S(2)}) %collective-permute-start.5) | collective-permute-done | bytes 16416 | tf_op jit(solution)/shard_map/ppermute | solution.py:267
  13.7 0.7 %pair_terms.6 = bf16[128,256]{1,0:T(8,128)(2,1)S(1)} custom-call(bf16[4,2,1024]{2,1,0:T(2,128)(2,1)S(1)} %collective-permute-done.5.rec_ref, bf16[512,256]{1,0:T(8,128)(2,1)S(1)} %get-tuple-element.19.band_ref, bf16[2,128,1024]{2,1,0:T(8,128)(2,1)S(1)} %get-tuple-element.20.kept_ref, f32[2,128,1]{2,1,0:T(8,128)S(1)} %get-tuple-element.21.energy_ref, ...), custom_call_target="tpu_custom_call" | custom-call | flops 134217728 | bytes 1048576 | tf_op jit(solution)/shard_map/pair_terms/pallas_call | solution.py:208
  14.4 1.8 %collective-permute-start.6 = (bf16[128,256]{1,0:T(8,128)(2,1)S(1)}, bf16[128,256]{1,0:T(8,128)(2,1)S(1)}, u32[]{:S(2)}, u32[]{:S(2)}) collective-permute-start(bf16[128,256]{1,0:T(8,128)(2,1)S(1)} %pair_terms.6), channel_id=1, source_target_pairs={{0,12},{4,8},{8,4},{12,0},{1,13},{5,9},{9,5},{13,1},{2,14},{6,10},... | collective-permute-start | bytes 196616 | tf_op jit(solution)/shard_map/ppermute | solution.py:264
  16.2 0.0 collective-permute-done.3.rec_ref
  16.2 0.7 %pair_terms.5 = bf16[128,256]{1,0:T(8,128)(2,1)S(1)} custom-call(bf16[4,2,1024]{2,1,0:T(2,128)(2,1)S(1)} %collective-permute-done.3.rec_ref, bf16[512,256]{1,0:T(8,128)(2,1)S(1)} %get-tuple-element.19.band_ref, bf16[2,128,1024]{2,1,0:T(8,128)(2,1)S(1)} %get-tuple-element.20.kept_ref, f32[2,128,1]{2,1,0:T(8,128)S(1)} %get-tuple-element.21.energy_ref, ...), custom_call_target="tpu_custom_call" | custom-call | flops 134217728 | bytes 1048576 | tf_op jit(solution)/shard_map/pair_terms/pallas_call | solution.py:208
  16.9 0.0 copy-start
  16.9 0.1 collective-permute-start.4
  17.0 0.7 %pair_terms.4 = f32[128,256]{1,0:T(8,128)S(1)} custom-call(bf16[4,2,1024]{2,1,0:T(2,128)(2,1)S(1)} %pad_maximum_fusion.rec_ref, bf16[512,256]{1,0:T(8,128)(2,1)S(1)} %get-tuple-element.19.band_ref, bf16[2,128,1024]{2,1,0:T(8,128)(2,1)S(1)} %get-tuple-element.20.kept_ref, f32[2,128,1]{2,1,0:T(8,128)S(1)} %get-tuple-element.21.energy_ref, ...), custom_call_target="tpu_custom_call" | custom-call | flops 134217728 | bytes 1048576 | tf_op jit(solution)/shard_map/pair_terms/pallas_call | solution.py:208
  17.6 0.0 collective-permute-done.8
  17.6 3.0 %collective-permute-done.6 = bf16[128,256]{1,0:T(8,128)(2,1)S(1)} collective-permute-done((bf16[128,256]{1,0:T(8,128)(2,1)S(1)}, bf16[128,256]{1,0:T(8,128)(2,1)S(1)}, u32[]{:S(2)}, u32[]{:S(2)}) %collective-permute-start.6) | collective-permute-done | bytes 65568 | tf_op jit(solution)/shard_map/ppermute | solution.py:264
  20.6 1.5 %collective-permute-done.4 = bf16[128,256]{1,0:T(8,128)(2,1)S(1)} collective-permute-done((bf16[128,256]{1,0:T(8,128)(2,1)S(1)}, bf16[128,256]{1,0:T(8,128)(2,1)S(1)}, u32[]{:S(2)}, u32[]{:S(2)}) %collective-permute-start.4) | collective-permute-done | bytes 65568 | tf_op jit(solution)/shard_map/ppermute | solution.py:264
  22.1 0.0 copy-done
  22.1 0.7 %convert_add_fusion = f32[128,256]{1,0:T(8,128)} fusion(bf16[128,256]{1,0:T(8,128)(2,1)S(1)} %collective-permute-done.8, bf16[128,256]{1,0:T(8,128)(2,1)S(1)} %collective-permute-done.6, bf16[128,256]{1,0:T(8,128)(2,1)S(1)} %collective-permute-done.4, f32[128,256]{1,0:T(8,128)S(1)} %copy-done, f32[128,256]{1,0:T(8,128)S(1)} %pair_terms.4), kind=kLoop, calls=%fused_computation | loop fusion | flops 229376 | bytes 589824 | tf_op jit(solution)/shard_map/add | solution.py:274
  (3 shorter events, 0.1 us)
Async XLA Ops:
  0.0 3.1 %copy-start.2 = (bf16[129]{0:T(256)(128)(2,1)S(1)}, bf16[129]{0:T(256)(128)(2,1)}, u32[]{:S(2)}) copy-start(bf16[129]{0:T(256)(128)(2,1)} %param.10) | copy-start | bytes 778
  0.0 5.4 %collective-permute-start.2 = (bf16[1,2,1024]{2,1,0:T(2,128)(2,1)}, bf16[1,2,1024]{2,1,0:T(2,128)(2,1)S(1)}, u32[]{:S(2)}, u32[]{:S(2)}) collective-permute-start(bf16[1,2,1024]{2,1,0:T(2,128)(2,1)} %bitcast.13), channel_id=1, source_target_pairs={{0,1},{1,0},{2,3},{3,2},{4,5},{5,4},{6,7},{7,6},{8,9},{9,8},{10,11... | collective-permute-start | bytes 12296 | tf_op jit(solution)/shard_map/ppermute | solution.py:233
  0.5 4.9 %collective-permute-start.1 = (bf16[1,2,1024]{2,1,0:T(2,128)(2,1)}, bf16[1,2,1024]{2,1,0:T(2,128)(2,1)S(1)}, u32[]{:S(2)}, u32[]{:S(2)}) collective-permute-start(bf16[1,2,1024]{2,1,0:T(2,128)(2,1)} %bitcast.14), channel_id=1, source_target_pairs={{0,2},{1,3},{2,0},{3,1},{4,6},{5,7},{6,4},{7,5},{8,10},{9,11},{10,... | collective-permute-start | bytes 12296 | tf_op jit(solution)/shard_map/ppermute | solution.py:233
  3.0 3.2 %collective-permute-start = (bf16[1,2,1024]{2,1,0:T(2,128)(2,1)}, bf16[1,2,1024]{2,1,0:T(2,128)(2,1)S(1)}, u32[]{:S(2)}, u32[]{:S(2)}) collective-permute-start(bf16[1,2,1024]{2,1,0:T(2,128)(2,1)} %bitcast.15), channel_id=1, source_target_pairs={{0,3},{1,2},{2,1},{3,0},{4,7},{5,6},{6,5},{7,4},{8,11},{9,10},{10,... | collective-permute-start | bytes 12296 | tf_op jit(solution)/shard_map/ppermute | solution.py:233
  5.4 0.9 %copy-start.1 = (bf16[2,1,1024]{2,0,1:T(2,128)(2,1)S(1)}, bf16[2,1,1024]{2,0,1:T(2,128)(2,1)}, u32[]{:S(2)}) copy-start(bf16[2,1,1024]{2,0,1:T(2,128)(2,1)} %param.9) | copy-start | bytes 12292
  6.3 4.3 %collective-permute-start.7 = (bf16[4,2,1024]{2,1,0:T(2,128)(2,1)S(1)}, bf16[4,2,1024]{2,1,0:T(2,128)(2,1)S(1)}, u32[]{:S(2)}, u32[]{:S(2)}) collective-permute-start(bf16[4,2,1024]{2,1,0:T(2,128)(2,1)S(1)} %pad_maximum_fusion.rec_ref), channel_id=1, source_target_pairs={{4,0},{0,4},{12,8},{8,12},{5,1},{1,5},{13,9},{9,13},{6,2},{2,6},{1... | collective-permute-start | bytes 49160 | tf_op jit(solution)/shard_map/ppermute | solution.py:267
  8.1 5.6 %collective-permute-start.5 = (bf16[4,2,1024]{2,1,0:T(2,128)(2,1)S(1)}, bf16[4,2,1024]{2,1,0:T(2,128)(2,1)S(1)}, u32[]{:S(2)}, u32[]{:S(2)}) collective-permute-start(bf16[4,2,1024]{2,1,0:T(2,128)(2,1)S(1)} %pad_maximum_fusion.rec_ref), channel_id=1, source_target_pairs={{12,0},{8,4},{4,8},{0,12},{13,1},{9,5},{5,9},{1,13},{14,2},{10,6},... | collective-permute-start | bytes 49160 | tf_op jit(solution)/shard_map/ppermute | solution.py:267
  10.5 5.7 %collective-permute-start.3 = (bf16[4,2,1024]{2,1,0:T(2,128)(2,1)S(1)}, bf16[4,2,1024]{2,1,0:T(2,128)(2,1)S(1)}, u32[]{:S(2)}, u32[]{:S(2)}) collective-permute-start(bf16[4,2,1024]{2,1,0:T(2,128)(2,1)S(1)} %pad_maximum_fusion.rec_ref), channel_id=1, source_target_pairs={{8,0},{12,4},{0,8},{4,12},{9,1},{13,5},{1,9},{5,13},{10,2},{14,6},... | collective-permute-start | bytes 49160 | tf_op jit(solution)/shard_map/ppermute | solution.py:267
  11.3 6.3 %collective-permute-start.8 = (bf16[128,256]{1,0:T(8,128)(2,1)S(1)}, bf16[128,256]{1,0:T(8,128)(2,1)S(1)}, u32[]{:S(2)}, u32[]{:S(2)}) collective-permute-start(bf16[128,256]{1,0:T(8,128)(2,1)S(1)} %pair_terms.7), channel_id=1, source_target_pairs={{0,4},{4,0},{8,12},{12,8},{1,5},{5,1},{9,13},{13,9},{2,6},{6,2},{1... | collective-permute-start | bytes 196616 | tf_op jit(solution)/shard_map/ppermute | solution.py:264
  14.4 6.2 %collective-permute-start.6 = (bf16[128,256]{1,0:T(8,128)(2,1)S(1)}, bf16[128,256]{1,0:T(8,128)(2,1)S(1)}, u32[]{:S(2)}, u32[]{:S(2)}) collective-permute-start(bf16[128,256]{1,0:T(8,128)(2,1)S(1)} %pair_terms.6), channel_id=1, source_target_pairs={{0,12},{4,8},{8,4},{12,0},{1,13},{5,9},{9,5},{13,1},{2,14},{6,10},... | collective-permute-start | bytes 196616 | tf_op jit(solution)/shard_map/ppermute | solution.py:264
  16.9 5.2 %copy-start = (f32[128,256]{1,0:T(8,128)S(1)}, f32[128,256]{1,0:T(8,128)}, u32[]{:S(2)}) copy-start(f32[128,256]{1,0:T(8,128)} %param.11) | copy-start | bytes 393220
  16.9 5.2 %collective-permute-start.4 = (bf16[128,256]{1,0:T(8,128)(2,1)S(1)}, bf16[128,256]{1,0:T(8,128)(2,1)S(1)}, u32[]{:S(2)}, u32[]{:S(2)}) collective-permute-start(bf16[128,256]{1,0:T(8,128)(2,1)S(1)} %pair_terms.5), channel_id=1, source_target_pairs={{0,8},{4,12},{8,0},{12,4},{1,9},{5,13},{9,1},{13,5},{2,10},{6,14},... | collective-permute-start | bytes 196616 | tf_op jit(solution)/shard_map/ppermute | solution.py:264
